TPU v7x, 256 devices: a whole 4x4x8 slice. The times are simulated.
256 devices in a mesh: seq: 64 (over y, z, core), dp: 4 (over x).
Axes of the slice: x: 4, y: 4, z: 8, core: 2. Of those that a mesh axis runs over, the one named last changes fastest.
Arguments:
- probe_vectors: bfloat16 [4, 8192, 2048], P('dp', 'seq'), may hold values from -6 to 6
- lookup_vectors: bfloat16 [4, 8192, 2048], P('dp', 'seq'), may hold values from -6 to 6
- content_vectors: bfloat16 [4, 8192, 2048], P('dp', 'seq'), may hold values from -6 to 6
- result_cotangent: bfloat16 [4, 8192, 2048], P('dp', 'seq'), may hold values from -25 to 25
- logit_softness: float32 [16], replicated, may hold values from 0.7 to 1.2
- block_grouping: int32 [4, 16, 64, 1], P('dp'), may hold values from 0 to 7, as said below
- neighborhood_span: int32 [16], replicated, may hold values from 32 to 128
Outputs:
- query_grad: bfloat16 [4, 8192, 2048], P('dp', 'seq')
- key_grad: bfloat16 [4, 8192, 2048], P('dp', 'seq')
- value_grad: bfloat16 [4, 8192, 2048], P('dp', 'seq')
- temper_grad: float32 [16], replicated
Inputs may be any that keep to these rules, and one draw needn't show every extreme that they name: `block_grouping`: within one document and head no cluster holds more than 12 blocks, and some cluster holds exactly 12. Index j of seq owns the clusters c of head h with (h * 8 + c) // 2 == j; of the 1 block of one index of seq, at most 1 have for one head clusters owned by one index of seq, and that many is reached.
All inputs are finite; a program needn't handle non-finite values.
Results may differ from a plain program's by a relative error of at most 0.0076.
Values may be sent and summed in bfloat16 or wider, within the bound.
A program may use at most 64 MiB of HBM per device.

v0:
```python
import math

import jax
import jax.numpy as jnp
from jax import lax
from jax.sharding import PartitionSpec as P

HD = 128
BLK = 128


blocked_score = -1e30


def shifted(value, axis, steps):
    count = lax.axis_size(axis)
    first, last = (max(0, -steps), min(count, count - steps))
    return lax.ppermute(value, axis, [(source, source + steps) for source in range(first, last)])


def lifted(array_in):
    return lax.optimization_barrier(array_in.astype(jnp.bfloat16)).astype(jnp.float32)


def head_major(tokens_in, block_len):
    token_count, feature_count = tokens_in.shape
    return tokens_in.reshape(
        token_count // block_len, block_len, feature_count // HD, HD
    ).transpose(2, 0, 1, 3)


def token_major(blocks_in):
    head_count, block_count, block_len, depth = blocks_in.shape
    return blocks_in.transpose(1, 2, 0, 3).reshape(1, block_count * block_len, head_count * depth)


def window_parts(query_block, prev_keys, prev_values, grad_block, usable, window_width, temper):
    block_len = query_block.shape[-2]
    inverse_root = 1.0 / math.sqrt(query_block.shape[-1])
    raw_scores = (
        jnp.einsum("...td,...sd->...ts", query_block, prev_keys, preferred_element_type=jnp.float32)
        * inverse_root
    )
    query_pos = lax.broadcasted_iota(jnp.int32, (block_len, block_len), 0)
    key_pos = lax.broadcasted_iota(jnp.int32, (block_len, block_len), 1)
    pair_mask = usable[..., None, None] & (
        key_pos > query_pos + block_len - window_width[..., None, None]
    )
    scores = temper[..., None, None] * raw_scores
    row_top = jnp.max(jnp.where(pair_mask, scores, blocked_score), axis=-1)
    weights = jnp.where(pair_mask, jnp.exp(scores - row_top[..., None]), 0.0)
    prob_grad = jnp.einsum(
        "...td,...sd->...ts", grad_block, prev_values, preferred_element_type=jnp.float32
    )
    return (
        raw_scores,
        pair_mask,
        prob_grad,
        row_top,
        jnp.sum(weights, axis=-1),
        jnp.sum(weights * prob_grad, axis=-1),
    )


def window_grads(
    raw_scores,
    pair_mask,
    prob_grad,
    query_block,
    prev_keys,
    grad_block,
    log_total,
    row_delta,
    temper,
):
    inverse_root = 1.0 / math.sqrt(query_block.shape[-1])
    scaling = (temper * inverse_root)[..., None, None]
    probability = jnp.where(
        pair_mask, jnp.exp(temper[..., None, None] * raw_scores - log_total[..., None]), 0.0
    )
    score_grad = probability * (prob_grad - row_delta[..., None])
    prob_low = probability.astype(jnp.bfloat16)
    grad_low = score_grad.astype(jnp.bfloat16)
    query_part = (
        jnp.einsum("...ts,...sd->...td", grad_low, prev_keys, preferred_element_type=jnp.float32)
        * scaling
    )
    key_part = (
        jnp.einsum("...ts,...td->...sd", grad_low, query_block, preferred_element_type=jnp.float32)
        * scaling
    )
    value_part = jnp.einsum(
        "...ts,...td->...sd", prob_low, grad_block, preferred_element_type=jnp.float32
    )
    temper_part = jnp.sum(score_grad * raw_scores, axis=(-2, -1))
    return (query_part, key_part, value_part, temper_part)


def cluster_pair(
    query_items,
    key_items,
    value_items,
    grad_items,
    live_items,
    temper,
    window_top,
    window_total,
    window_mass,
):
    item_count, block_len, depth = query_items.shape
    row_count = item_count * block_len
    group_rows = 4 * block_len
    inverse_root = 1.0 / math.sqrt(depth)
    scaling = temper * inverse_root
    query_rows = query_items.reshape(row_count, depth)
    key_rows = key_items.reshape(row_count, depth)
    value_rows = value_items.reshape(row_count, depth)
    grad_rows = grad_items.reshape(row_count, depth)
    key_item = jnp.arange(row_count) // block_len
    key_token = jnp.arange(row_count) % block_len
    live_rows = jnp.repeat(live_items, block_len)
    top_rows = window_top.reshape(row_count)
    total_rows = window_total.reshape(row_count)
    mass_rows = window_mass.reshape(row_count)

    def group_step(carry, start_row):
        key_acc, value_acc, temper_acc = carry
        query_group = lax.dynamic_slice_in_dim(query_rows, start_row, group_rows, 0)
        grad_group = lax.dynamic_slice_in_dim(grad_rows, start_row, group_rows, 0)
        group_live = lax.dynamic_slice_in_dim(live_rows, start_row, group_rows, 0)
        group_top = lax.dynamic_slice_in_dim(top_rows, start_row, group_rows, 0)
        group_total = lax.dynamic_slice_in_dim(total_rows, start_row, group_rows, 0)
        group_mass = lax.dynamic_slice_in_dim(mass_rows, start_row, group_rows, 0)
        query_item = (start_row + jnp.arange(group_rows)) // block_len
        query_token = jnp.arange(group_rows) % block_len
        earlier = (key_item[None, :] < query_item[:, None]) | (
            key_item[None, :] == query_item[:, None]
        ) & (key_token[None, :] <= query_token[:, None])
        pair_mask = group_live[:, None] & live_rows[None, :] & earlier
        raw_scores = (
            lax.dot_general(
                query_group, key_rows, (((1,), (1,)), ((), ())), preferred_element_type=jnp.float32
            )
            * inverse_root
        )
        scores = temper * raw_scores
        row_top = jnp.maximum(
            jnp.max(jnp.where(pair_mask, scores, blocked_score), axis=1), group_top
        )
        weights = jnp.where(pair_mask, jnp.exp(scores - row_top[:, None]), 0.0)
        row_total = jnp.sum(weights, axis=1) + group_total * jnp.exp(group_top - row_top)
        log_total = row_top + jnp.log(jnp.where(group_live, row_total, 1.0))
        probability = jnp.where(pair_mask, jnp.exp(scores - log_total[:, None]), 0.0)
        prob_grad = lax.dot_general(
            grad_group, value_rows, (((1,), (1,)), ((), ())), preferred_element_type=jnp.float32
        )
        row_delta = jnp.sum(probability * prob_grad, axis=1) + group_mass * jnp.exp(
            group_top - log_total
        )
        score_grad = probability * (prob_grad - row_delta[:, None])
        prob_low = probability.astype(jnp.bfloat16)
        grad_low = score_grad.astype(jnp.bfloat16)
        query_part = jnp.dot(grad_low, key_rows, preferred_element_type=jnp.float32) * scaling
        key_acc = (
            key_acc
            + lax.dot_general(
                grad_low, query_group, (((0,), (0,)), ((), ())), preferred_element_type=jnp.float32
            )
            * scaling
        )
        value_acc = value_acc + lax.dot_general(
            prob_low, grad_group, (((0,), (0,)), ((), ())), preferred_element_type=jnp.float32
        )
        temper_acc = temper_acc + jnp.sum(score_grad * raw_scores)
        return ((key_acc, value_acc, temper_acc), (query_part, log_total, row_delta))

    start_rows = jnp.arange(item_count // 4) * group_rows
    initial = (
        jnp.zeros((row_count, depth), jnp.float32),
        jnp.zeros((row_count, depth), jnp.float32),
        jnp.zeros((), jnp.float32),
    )
    (key_acc, value_acc, temper_acc), (query_part, log_total, row_delta) = lax.scan(
        group_step, initial, start_rows
    )
    return (
        query_part.reshape(item_count, block_len, depth),
        log_total.reshape(item_count, block_len),
        row_delta.reshape(item_count, block_len),
        key_acc.reshape(item_count, block_len, depth),
        value_acc.reshape(item_count, block_len, depth),
        temper_acc,
    )


def shards(
    probe_vectors,
    lookup_vectors,
    content_vectors,
    result_cotangent,
    logit_softness,
    block_grouping,
    neighborhood_span,
):
    seq_count = lax.axis_size("seq")
    position = lax.axis_index("seq")
    tokens = probe_vectors.shape[1]
    head_count = probe_vectors.shape[2] // HD
    local_blocks = tokens // BLK
    block_count = local_blocks * seq_count
    cluster_count = max(1, block_count // 8)
    capacity = min(12, block_count)
    owned_pairs = cluster_count * head_count // seq_count
    group_count = cluster_count // owned_pairs
    per_peer = max(1, local_blocks // group_count)
    cluster_ids = block_grouping[0, :, :, 0]
    query_home = head_major(probe_vectors[0], BLK)
    key_home = head_major(lookup_vectors[0], BLK)
    value_home = head_major(content_vectors[0], BLK)
    grad_home = head_major(result_cotangent[0], BLK)
    last_block = (lookup_vectors[0, tokens - BLK :], content_vectors[0, tokens - BLK :])
    prev_key_rows, prev_value_rows = shifted((last_block[0], last_block[1]), "seq", 1)
    prev_keys = jnp.concatenate([head_major(prev_key_rows, BLK), key_home[:, :-1]], axis=1)
    prev_values = jnp.concatenate([head_major(prev_value_rows, BLK), value_home[:, :-1]], axis=1)
    first_block = position * local_blocks
    before = jnp.concatenate(
        [jnp.full((head_count, 1), -1, jnp.int32), cluster_ids[:, :-1]], axis=1
    )
    my_ids = lax.dynamic_slice_in_dim(cluster_ids, first_block, local_blocks, 1)
    peer_index = jnp.arange(seq_count)
    peer_head = peer_index * owned_pairs // cluster_count
    slot_range = jnp.arange(per_peer)
    local_range = jnp.arange(local_blocks)
    owner_index = (jnp.arange(head_count)[:, None] * cluster_count + my_ids) // owned_pairs
    peer_ids = jnp.take(my_ids, peer_head, axis=0)
    goes = (peer_head[:, None] * cluster_count + peer_ids) // owned_pairs == peer_index[:, None]
    send_rank = jnp.cumsum(goes.astype(jnp.int32), axis=1) - 1
    send_pick = goes[:, None, :] & (send_rank[:, None, :] == slot_range[None, :, None])
    send_block = jnp.sum(jnp.where(send_pick, local_range[None, None, :], 0), axis=2)
    send_flat = peer_head[:, None] * local_blocks + send_block
    home_rank = jnp.take_along_axis(send_rank, owner_index, axis=0)
    home_pos = owner_index * per_peer + home_rank
    pair_index = position * owned_pairs + jnp.arange(owned_pairs)
    split_for_couple = pair_index // cluster_count
    pair_cluster = pair_index % cluster_count
    my_head = position * owned_pairs // cluster_count
    split_numbers = jnp.take(cluster_ids, my_head, axis=0)
    member = split_numbers[None, :] == pair_cluster[:, None]
    member_rank = jnp.cumsum(member.astype(jnp.int32), axis=1) - 1
    member_count = jnp.sum(member.astype(jnp.int32), axis=1)
    picked = member[:, None, :] & (member_rank[:, None, :] == jnp.arange(capacity)[None, :, None])
    member_block = jnp.sum(jnp.where(picked, jnp.arange(block_count)[None, None, :], 0), axis=2)
    live_members = jnp.arange(capacity)[None, :] < member_count[:, None]
    mine = (my_head * cluster_count + split_numbers) // owned_pairs == position
    mine_grid = mine.reshape(seq_count, local_blocks)
    recv_rank = jnp.cumsum(mine_grid.astype(jnp.int32), axis=1) - 1
    recv_pos = (peer_index[:, None] * per_peer + recv_rank).reshape(block_count)
    member_pos = jnp.take(recv_pos, member_block)
    head_before = jnp.take(before, my_head, axis=0)
    pair_before = jnp.take(head_before, member_block)
    pair_usable = live_members & (member_block >= 1) & (pair_before != pair_cluster[:, None])
    couple_softness = jnp.take(logit_softness, split_for_couple)
    pair_width = jnp.take(neighborhood_span, split_for_couple)
    pair_onehot = (split_for_couple[:, None] == jnp.arange(head_count)[None, :]).astype(jnp.float32)
    slot_pair = my_head * cluster_count + split_numbers - position * owned_pairs
    same_cluster = split_numbers[:, None] == split_numbers[None, :]
    earlier_block = jnp.arange(block_count)[None, :] < jnp.arange(block_count)[:, None]
    slot_rank = jnp.sum((same_cluster & earlier_block).astype(jnp.int32), axis=1)
    back_pos = jnp.clip(slot_pair, 0, owned_pairs - 1) * capacity + jnp.clip(
        slot_rank, 0, capacity - 1
    )
    back_grid = back_pos.reshape(seq_count, local_blocks)
    back_pick = mine_grid[:, None, :] & (recv_rank[:, None, :] == slot_range[None, :, None])
    back_flat = jnp.sum(jnp.where(back_pick, back_grid[:, None, :], 0), axis=2)

    def to_peers(array_in):
        flat = array_in.reshape((head_count * local_blocks,) + array_in.shape[2:])
        return jnp.take(flat, send_flat, axis=0)

    def members(array_in):
        flat = array_in.reshape((seq_count * per_peer,) + array_in.shape[2:])
        return jnp.take(flat, member_pos, axis=0)

    def to_owner(array_in):
        flat = array_in.reshape((owned_pairs * capacity,) + array_in.shape[2:])
        return jnp.take(flat, back_flat, axis=0)

    def from_peers(array_in):
        flat = array_in.reshape((seq_count * per_peer,) + array_in.shape[2:])
        return jnp.take(flat, home_pos, axis=0)

    arrived = (
        lax.all_to_all(to_peers(query_home), "seq", split_axis=0, concat_axis=0, tiled=True),
        lax.all_to_all(to_peers(key_home), "seq", split_axis=0, concat_axis=0, tiled=True),
        lax.all_to_all(to_peers(value_home), "seq", split_axis=0, concat_axis=0, tiled=True),
        lax.all_to_all(to_peers(grad_home), "seq", split_axis=0, concat_axis=0, tiled=True),
        lax.all_to_all(to_peers(prev_keys), "seq", split_axis=0, concat_axis=0, tiled=True),
        lax.all_to_all(to_peers(prev_values), "seq", split_axis=0, concat_axis=0, tiled=True),
    )
    query_m, key_m, value_m, grad_m, prevk_m, prevv_m = [members(item_in) for item_in in arrived]

    def owner_pair(pair_inputs):
        query_i, key_i, value_i, grad_i, prevk_i, prevv_i, usable_i, live_i, temper_i, width_i = (
            pair_inputs
        )
        raw_w, mask_w, pgrad_w, top_w, total_w, mass_w = window_parts(
            query_i, prevk_i, prevv_i, grad_i, usable_i, width_i, temper_i
        )
        query_c, log_total, row_delta, key_c, value_c, temper_c = cluster_pair(
            query_i, key_i, value_i, grad_i, live_i, temper_i, top_w, total_w, mass_w
        )
        query_w, key_w, value_w, temper_w = window_grads(
            raw_w, mask_w, pgrad_w, query_i, prevk_i, grad_i, log_total, row_delta, temper_i
        )
        query_out = (lifted(query_c) + lifted(query_w)).astype(jnp.bfloat16)
        return (
            query_out,
            key_c.astype(jnp.bfloat16),
            value_c.astype(jnp.bfloat16),
            key_w.astype(jnp.bfloat16),
            value_w.astype(jnp.bfloat16),
            temper_c + jnp.sum(temper_w),
        )

    owner_results = lax.map(
        owner_pair,
        (
            query_m,
            key_m,
            value_m,
            grad_m,
            prevk_m,
            prevv_m,
            pair_usable,
            live_members,
            couple_softness,
            pair_width,
        ),
    )
    returned = (
        lax.all_to_all(to_owner(owner_results[0]), "seq", split_axis=0, concat_axis=0, tiled=True),
        lax.all_to_all(to_owner(owner_results[1]), "seq", split_axis=0, concat_axis=0, tiled=True),
        lax.all_to_all(to_owner(owner_results[2]), "seq", split_axis=0, concat_axis=0, tiled=True),
        lax.all_to_all(to_owner(owner_results[3]), "seq", split_axis=0, concat_axis=0, tiled=True),
        lax.all_to_all(to_owner(owner_results[4]), "seq", split_axis=0, concat_axis=0, tiled=True),
    )
    query_out = from_peers(returned[0])
    key_cluster = from_peers(returned[1])
    value_cluster = from_peers(returned[2])
    key_window = from_peers(returned[3])
    value_window = from_peers(returned[4])
    temper_local = jnp.sum(owner_results[5][:, None] * pair_onehot, axis=0)
    edge_keys, edge_values = shifted((key_window[:, 0], value_window[:, 0]), "seq", -1)
    key_next = jnp.concatenate([key_window[:, 1:], edge_keys[:, None]], axis=1)
    value_next = jnp.concatenate([value_window[:, 1:], edge_values[:, None]], axis=1)
    key_out = (key_cluster.astype(jnp.float32) + key_next.astype(jnp.float32)).astype(jnp.bfloat16)
    value_out = (value_cluster.astype(jnp.float32) + value_next.astype(jnp.float32)).astype(
        jnp.bfloat16
    )
    temper_total = lax.psum(temper_local, ("seq", "dp"))
    temper_grad = temper_total / (lax.axis_size("dp") * tokens * seq_count)
    return (token_major(query_out), token_major(key_out), token_major(value_out), temper_grad)


def solution(mesh):
    in_specs = (
        P("dp", "seq", None),
        P("dp", "seq", None),
        P("dp", "seq", None),
        P("dp", "seq", None),
        P(),
        P("dp", None, None, None),
        P(),
    )
    out_specs = (P("dp", "seq", None), P("dp", "seq", None), P("dp", "seq", None), P())
    return jax.shard_map(shards, mesh=mesh, in_specs=in_specs, out_specs=out_specs, check_vma=False)
```

profile of v0, /device:TPU:1, one launch (start us, length us, event | category | flops | bytes accessed | tf_op | source)
XLA Modules:
  0.0 998.4 jit_solution(14988729749340232094)
XLA Ops:
  2.7 4.9 collective-permute-start
  32.0 5.7 fusion.71
  37.8 62.3 %all_to_all.55 = bf16[64,1,128,128]{3,2,1,0:T(8,128)(2,1)} all-to-all(bf16[64,1,128,128]{3,2,1,0:T(8,128)(2,1)S(1)} %get-tuple-element.938), channel_id=1, replica_groups=mesh['seq'=64,'dp'=4] {'seq'}, dimensions={0} | all-to-all | bytes 4194304 | tf_op jit(solution)/shard_map/all_to_all | solution.py:293
  100.1 56.9 %all_to_all.56 = bf16[64,1,128,128]{3,2,1,0:T(8,128)(2,1)} all-to-all(bf16[64,1,128,128]{3,2,1,0:T(8,128)(2,1)S(1)} %get-tuple-element.937), channel_id=1, replica_groups=mesh['seq'=64,'dp'=4] {'seq'}, dimensions={0} | all-to-all | bytes 4194304 | tf_op jit(solution)/shard_map/all_to_all | solution.py:294
  157.0 56.9 %all_to_all.57 = bf16[64,1,128,128]{3,2,1,0:T(8,128)(2,1)} all-to-all(bf16[64,1,128,128]{3,2,1,0:T(8,128)(2,1)S(1)} %get-tuple-element.936), channel_id=1, replica_groups=mesh['seq'=64,'dp'=4] {'seq'}, dimensions={0} | all-to-all | bytes 4194304 | tf_op jit(solution)/shard_map/all_to_all | solution.py:298
  214.0 56.9 %all_to_all.58 = bf16[64,1,128,128]{3,2,1,0:T(8,128)(2,1)} all-to-all(bf16[64,1,128,128]{3,2,1,0:T(8,128)(2,1)S(1)} %get-tuple-element.935), channel_id=1, replica_groups=mesh['seq'=64,'dp'=4] {'seq'}, dimensions={0} | all-to-all | bytes 4194304 | tf_op jit(solution)/shard_map/all_to_all | solution.py:297
  270.9 56.9 %all_to_all.59 = bf16[64,1,128,128]{3,2,1,0:T(8,128)(2,1)} all-to-all(bf16[64,1,128,128]{3,2,1,0:T(8,128)(2,1)S(1)} %get-tuple-element.934), channel_id=1, replica_groups=mesh['seq'=64,'dp'=4] {'seq'}, dimensions={0} | all-to-all | bytes 4194304 | tf_op jit(solution)/shard_map/all_to_all | solution.py:296
  327.8 17.1 %all-to-all-start.5 = ((bf16[64,1,128,128]{3,2,1,0:T(8,128)(2,1)}), bf16[64,1,128,128]{3,2,1,0:T(8,128)(2,1)S(1)}, u32[]{:S(2)}, u32[]{:S(2)}) async-start(bf16[64,1,128,128]{3,2,1,0:T(8,128)(2,1)} %get-tuple-element.933), calls=%async_computation.5 | async-start | bytes 4194304 | tf_op jit(solution)/shard_map/all_to_all | solution.py:295
  367.6 28.4 %all-to-all-done.5 = bf16[64,1,128,128]{3,2,1,0:T(8,128)(2,1)S(1)} async-done(((bf16[64,1,128,128]{3,2,1,0:T(8,128)(2,1)}), bf16[64,1,128,128]{3,2,1,0:T(8,128)(2,1)S(1)}, u32[]{:S(2)}, u32[]{:S(2)}) %all-to-all-start.5) | async-done | bytes 2097184 | tf_op jit(solution)/shard_map/all_to_all | solution.py:295
  397.7 4.4 broadcast_select_fusion
  402.1 238.5 %while.78 = (s32[]{:T(128)}, bf16[2,12,128,128]{3,2,1,0:T(8,128)(2,1)}, bf16[2,12,128,128]{3,2,1,0:T(8,128)(2,1)}, bf16[2,12,128,128]{3,2,1,0:T(8,128)(2,1)}, bf...) while((s32[]{:T(128)}, ...), condition=%wide.region_14.19_spmd, body=%wide.region_3.18_spmd.sunk | while | flops 1333505792 | bytes 114306376 | solution.py:325
  419.3 89.3 %while.79 = (s32[]{:T(128)}, f32[1536,128]{1,0:T(8,128)}, f32[1536,128]{1,0:T(8,128)}, f32[]{:T(128)}, bf16[3,512,128]{2,1,0:T(8,128)(2,1)}, /*index=5*/f32[3,51...) while((s32[]{:T(128)}, f32[1536,128]{1,0:T(8,128)}, ...), condition=%wide.region_12.16_spmd.clone.clone, body=%wide.region_7.15_spmd.clone.clone.sunk | while | flops 1074561024 | bytes 77815136 | solution.py:183
  435.2 3.4 multiply_reduce_fusion.11
  439.4 3.7 convolution_add_fusion.2
  464.8 3.4 multiply_reduce_fusion.11
  469.0 4.0 convolution_add_fusion.2
  494.6 3.4 multiply_reduce_fusion.11
  498.8 4.0 convolution_add_fusion.2
  538.6 89.3 %while.79 = (s32[]{:T(128)}, f32[1536,128]{1,0:T(8,128)}, f32[1536,128]{1,0:T(8,128)}, f32[]{:T(128)}, bf16[3,512,128]{2,1,0:T(8,128)(2,1)}, /*index=5*/f32[3,51...) while((s32[]{:T(128)}, f32[1536,128]{1,0:T(8,128)}, ...), condition=%wide.region_12.16_spmd.clone.clone, body=%wide.region_7.15_spmd.clone.clone.sunk | while | flops 1074561024 | bytes 77815136 | solution.py:183
  554.4 3.4 multiply_reduce_fusion.11
  558.6 3.7 convolution_add_fusion.2
  588.2 4.0 convolution_add_fusion.2
  618.0 4.0 convolution_add_fusion.2
  646.1 3.6 fusion.69
  649.6 56.8 %all_to_all.60 = bf16[64,1,128,128]{3,2,1,0:T(8,128)(2,1)} all-to-all(bf16[64,1,128,128]{3,2,1,0:T(8,128)(2,1)S(1)} %get-tuple-element.926), channel_id=1, replica_groups=mesh['seq'=64,'dp'=4] {'seq'}, dimensions={0} | all-to-all | bytes 4194304 | tf_op jit(solution)/shard_map/all_to_all | solution.py:341
  706.5 6.2 all-to-all-start.8
  720.3 5.4 bitcast_select_fusion.1
  725.7 38.0 %all-to-all-done.8 = bf16[64,1,128,128]{3,2,1,0:T(8,128)(2,1)} async-done(((bf16[64,1,128,128]{3,2,1,0:T(8,128)(2,1)}), bf16[64,1,128,128]{3,2,1,0:T(8,128)(2,1)}, u32[]{:S(2)}, u32[]{:S(2)}) %all-to-all-start.8) | async-done | bytes 2097184 | tf_op jit(solution)/shard_map/all_to_all | solution.py:344
  763.8 57.1 %all_to_all.61 = bf16[64,1,128,128]{3,2,1,0:T(8,128)(2,1)} all-to-all(bf16[64,1,128,128]{3,2,1,0:T(8,128)(2,1)} %get-tuple-element.920), channel_id=1, replica_groups=mesh['seq'=64,'dp'=4] {'seq'}, dimensions={0} | all-to-all | bytes 4194304 | tf_op jit(solution)/shard_map/all_to_all | solution.py:345
  820.9 56.9 %all_to_all.62 = bf16[64,1,128,128]{3,2,1,0:T(8,128)(2,1)} all-to-all(bf16[64,1,128,128]{3,2,1,0:T(8,128)(2,1)S(1)} %get-tuple-element.921), channel_id=1, replica_groups=mesh['seq'=64,'dp'=4] {'seq'}, dimensions={0} | all-to-all | bytes 4194304 | tf_op jit(solution)/shard_map/all_to_all | solution.py:342
  877.8 6.0 all-to-all-start.9
  901.0 87.1 %psum.7 = f32[16]{0:T(128)S(1)} all-reduce(f32[16]{0:T(128)S(1)} %fusion.87), channel_id=1, replica_groups=mesh['seq'=64,'dp'=4] {'seq','dp'}, use_global_device_ids=true, to_apply=%region_17.24 | all-reduce | flops 16 | bytes 128 | tf_op jit(solution)/shard_map/psum | solution.py:360
  (573 shorter events, 272.7 us)
Async XLA Ops:
  0.6 349.0 %copy-start = (f32[16]{0:T(128)S(1)}, f32[16]{0:T(128)}, u32[]{:S(2)}) copy-start(f32[16]{0:T(128)} %param.27) | copy-start | bytes 196
  2.7 22.3 %collective-permute-start = (bf16[128,2048]{0,1:T(8,128)(2,1)}, bf16[128,2048]{0,1:T(8,128)(2,1)}, u32[]{:S(2)}, u32[]{:S(2)}) collective-permute-start(bf16[128,2048]{0,1:T(8,128)(2,1)} %bitcast.54), channel_id=1, source_target_pairs={{0,4},{4,8},{8,12},{12,16},{16,20},{20,24},{24,28},{28,32},{32,36}... | collective-permute-start | bytes 1572872 | tf_op jit(solution)/shard_map/ppermute | solution.py:18
  9.7 18.9 %collective-permute-start.1 = (bf16[128,2048]{0,1:T(8,128)(2,1)}, bf16[128,2048]{0,1:T(8,128)(2,1)}, u32[]{:S(2)}, u32[]{:S(2)}) collective-permute-start(bf16[128,2048]{0,1:T(8,128)(2,1)} %bitcast.64), channel_id=1, source_target_pairs={{0,4},{4,8},{8,12},{12,16},{16,20},{20,24},{24,28},{28,32},{32,36}... | collective-permute-start | bytes 1572872 | tf_op jit(solution)/shard_map/ppermute | solution.py:18
  14.2 15.6 %copy-start.37 = (s32[1024]{0:T(1024)}, s32[1024]{0:T(1024)S(1)}, u32[]{:S(2)}) copy-start(s32[1024]{0:T(1024)S(1)} %pad_clamp_fusion.6) | copy-start | bytes 12292
  327.8 17.7 %copy-start.35 = (s32[1,16,64,1]{2,3,1,0:T(1,128)S(1)}, s32[1,16,64,1]{2,3,1,0:T(1,128)}, u32[]{:S(2)}) copy-start(s32[1,16,64,1]{2,3,1,0:T(1,128)} %param.28) | copy-start | bytes 12292
  327.8 68.3 %all-to-all-start.5 = ((bf16[64,1,128,128]{3,2,1,0:T(8,128)(2,1)}), bf16[64,1,128,128]{3,2,1,0:T(8,128)(2,1)S(1)}, u32[]{:S(2)}, u32[]{:S(2)}) async-start(bf16[64,1,128,128]{3,2,1,0:T(8,128)(2,1)} %get-tuple-element.933), calls=%async_computation.5 | async-start | bytes 4194304 | tf_op jit(solution)/shard_map/all_to_all | solution.py:295
  402.1 11.4 %copy-start.42 = (pred[2,12]{1,0:T(4,128)(4,1)}, pred[2,12]{1,0:T(4,128)(4,1)S(1)}, u32[]{:S(2)}) copy-start(pred[2,12]{1,0:T(4,128)(4,1)S(1)} %get-tuple-element.1363) | copy-start | bytes 76 | tf_op jit(solution)/shard_map/while
  423.1 12.1 %copy-start.31 = (pred[512]{0:T(512)(128)(4,1)}, pred[512]{0:T(512)(128)(4,1)S(1)}, u32[]{:S(2)}) copy-start(pred[512]{0:T(512)(128)(4,1)S(1)} %dynamic_slice.240) | copy-start | bytes 1540 | tf_op jit(solution)/shard_map/while/body/eval_jaxpr/while
  423.6 11.5 %copy-start.13 = (s32[512]{0:T(512)}, s32[512]{0:T(512)S(1)}, u32[]{:S(2)}) copy-start(s32[512]{0:T(512)S(1)} %get-tuple-element.1237) | copy-start | bytes 6148 | tf_op jit(solution)/shard_map/while/body/eval_jaxpr/while
  423.7 11.5 %copy-start.7 = (s32[1536]{0:T(1024)}, s32[1536]{0:T(1024)S(1)}, u32[]{:S(2)}) copy-start(s32[1536]{0:T(1024)S(1)} %get-tuple-element.1238) | copy-start | bytes 18436 | tf_op jit(solution)/shard_map/while/body/eval_jaxpr/while
  424.3 10.8 %copy-start.15 = (pred[1536]{0:T(1024)(128)(4,1)}, pred[1536]{0:T(1024)(128)(4,1)S(1)}, u32[]{:S(2)}) copy-start(pred[1536]{0:T(1024)(128)(4,1)S(1)} %broadcast_bitcast_fusion.5) | copy-start | bytes 4612 | tf_op jit(solution)/shard_map/while/body/eval_jaxpr/while
  452.6 12.0 %copy-start.31 = (pred[512]{0:T(512)(128)(4,1)}, pred[512]{0:T(512)(128)(4,1)S(1)}, u32[]{:S(2)}) copy-start(pred[512]{0:T(512)(128)(4,1)S(1)} %dynamic_slice.240) | copy-start | bytes 1540 | tf_op jit(solution)/shard_map/while/body/eval_jaxpr/while
  453.2 11.5 %copy-start.13 = (s32[512]{0:T(512)}, s32[512]{0:T(512)S(1)}, u32[]{:S(2)}) copy-start(s32[512]{0:T(512)S(1)} %get-tuple-element.1237) | copy-start | bytes 6148 | tf_op jit(solution)/shard_map/while/body/eval_jaxpr/while
  453.3 11.5 %copy-start.7 = (s32[1536]{0:T(1024)}, s32[1536]{0:T(1024)S(1)}, u32[]{:S(2)}) copy-start(s32[1536]{0:T(1024)S(1)} %get-tuple-element.1238) | copy-start | bytes 18436 | tf_op jit(solution)/shard_map/while/body/eval_jaxpr/while
  482.5 12.0 %copy-start.31 = (pred[512]{0:T(512)(128)(4,1)}, pred[512]{0:T(512)(128)(4,1)S(1)}, u32[]{:S(2)}) copy-start(pred[512]{0:T(512)(128)(4,1)S(1)} %dynamic_slice.240) | copy-start | bytes 1540 | tf_op jit(solution)/shard_map/while/body/eval_jaxpr/while
  483.1 11.4 %copy-start.13 = (s32[512]{0:T(512)}, s32[512]{0:T(512)S(1)}, u32[]{:S(2)}) copy-start(s32[512]{0:T(512)S(1)} %get-tuple-element.1237) | copy-start | bytes 6148 | tf_op jit(solution)/shard_map/while/body/eval_jaxpr/while
  483.1 11.4 %copy-start.7 = (s32[1536]{0:T(1024)}, s32[1536]{0:T(1024)S(1)}, u32[]{:S(2)}) copy-start(s32[1536]{0:T(1024)S(1)} %get-tuple-element.1238) | copy-start | bytes 18436 | tf_op jit(solution)/shard_map/while/body/eval_jaxpr/while
  521.3 11.4 %copy-start.42 = (pred[2,12]{1,0:T(4,128)(4,1)}, pred[2,12]{1,0:T(4,128)(4,1)S(1)}, u32[]{:S(2)}) copy-start(pred[2,12]{1,0:T(4,128)(4,1)S(1)} %get-tuple-element.1363) | copy-start | bytes 76 | tf_op jit(solution)/shard_map/while
  542.3 12.1 %copy-start.31 = (pred[512]{0:T(512)(128)(4,1)}, pred[512]{0:T(512)(128)(4,1)S(1)}, u32[]{:S(2)}) copy-start(pred[512]{0:T(512)(128)(4,1)S(1)} %dynamic_slice.240) | copy-start | bytes 1540 | tf_op jit(solution)/shard_map/while/body/eval_jaxpr/while
  542.9 11.5 %copy-start.13 = (s32[512]{0:T(512)}, s32[512]{0:T(512)S(1)}, u32[]{:S(2)}) copy-start(s32[512]{0:T(512)S(1)} %get-tuple-element.1237) | copy-start | bytes 6148 | tf_op jit(solution)/shard_map/while/body/eval_jaxpr/while
  542.9 11.5 %copy-start.7 = (s32[1536]{0:T(1024)}, s32[1536]{0:T(1024)S(1)}, u32[]{:S(2)}) copy-start(s32[1536]{0:T(1024)S(1)} %get-tuple-element.1238) | copy-start | bytes 18436 | tf_op jit(solution)/shard_map/while/body/eval_jaxpr/while
  543.6 10.8 %copy-start.15 = (pred[1536]{0:T(1024)(128)(4,1)}, pred[1536]{0:T(1024)(128)(4,1)S(1)}, u32[]{:S(2)}) copy-start(pred[1536]{0:T(1024)(128)(4,1)S(1)} %broadcast_bitcast_fusion.5) | copy-start | bytes 4612 | tf_op jit(solution)/shard_map/while/body/eval_jaxpr/while
  571.9 12.0 %copy-start.31 = (pred[512]{0:T(512)(128)(4,1)}, pred[512]{0:T(512)(128)(4,1)S(1)}, u32[]{:S(2)}) copy-start(pred[512]{0:T(512)(128)(4,1)S(1)} %dynamic_slice.240) | copy-start | bytes 1540 | tf_op jit(solution)/shard_map/while/body/eval_jaxpr/while
  572.5 11.5 %copy-start.13 = (s32[512]{0:T(512)}, s32[512]{0:T(512)S(1)}, u32[]{:S(2)}) copy-start(s32[512]{0:T(512)S(1)} %get-tuple-element.1237) | copy-start | bytes 6148 | tf_op jit(solution)/shard_map/while/body/eval_jaxpr/while
  572.5 11.5 %copy-start.7 = (s32[1536]{0:T(1024)}, s32[1536]{0:T(1024)S(1)}, u32[]{:S(2)}) copy-start(s32[1536]{0:T(1024)S(1)} %get-tuple-element.1238) | copy-start | bytes 18436 | tf_op jit(solution)/shard_map/while/body/eval_jaxpr/while
  601.8 12.0 %copy-start.31 = (pred[512]{0:T(512)(128)(4,1)}, pred[512]{0:T(512)(128)(4,1)S(1)}, u32[]{:S(2)}) copy-start(pred[512]{0:T(512)(128)(4,1)S(1)} %dynamic_slice.240) | copy-start | bytes 1540 | tf_op jit(solution)/shard_map/while/body/eval_jaxpr/while
  602.3 11.4 %copy-start.13 = (s32[512]{0:T(512)}, s32[512]{0:T(512)S(1)}, u32[]{:S(2)}) copy-start(s32[512]{0:T(512)S(1)} %get-tuple-element.1237) | copy-start | bytes 6148 | tf_op jit(solution)/shard_map/while/body/eval_jaxpr/while
  602.4 11.4 %copy-start.7 = (s32[1536]{0:T(1024)}, s32[1536]{0:T(1024)S(1)}, u32[]{:S(2)}) copy-start(s32[1536]{0:T(1024)S(1)} %get-tuple-element.1238) | copy-start | bytes 18436 | tf_op jit(solution)/shard_map/while/body/eval_jaxpr/while
  706.5 57.3 %all-to-all-start.8 = ((bf16[64,1,128,128]{3,2,1,0:T(8,128)(2,1)}), bf16[64,1,128,128]{3,2,1,0:T(8,128)(2,1)}, u32[]{:S(2)}, u32[]{:S(2)}) async-start(bf16[64,1,128,128]{3,2,1,0:T(8,128)(2,1)} %get-tuple-element.925), calls=%async_computation.8 | async-start | bytes 4194304 | tf_op jit(solution)/shard_map/all_to_all | solution.py:344
  877.8 113.0 %all-to-all-start.9 = ((bf16[64,1,128,128]{3,2,1,0:T(8,128)(2,1)}), bf16[64,1,128,128]{3,2,1,0:T(8,128)(2,1)S(1)}, u32[]{:S(2)}, u32[]{:S(2)}) async-start(bf16[64,1,128,128]{3,2,1,0:T(8,128)(2,1)} %get-tuple-element.919), calls=%async_computation.9 | async-start | bytes 4194304 | tf_op jit(solution)/shard_map/all_to_all | solution.py:343
  896.6 97.0 %collective-permute-start.2 = (bf16[16,128,128]{2,1,0:T(8,128)(2,1)}, bf16[16,128,128]{2,1,0:T(8,128)(2,1)}, u32[]{:S(2)}, u32[]{:S(2)}) collective-permute-start(bf16[16,128,128]{2,1,0:T(8,128)(2,1)} %get-tuple-element.923), channel_id=1, source_target_pairs={{4,0},{8,4},{12,8},{16,12},{20,16},{24,20},{28,24},{32,28},{36,32}... | collective-permute-start | bytes 1572872 | tf_op jit(solution)/shard_map/ppermute | solution.py:18
  899.0 94.6 %collective-permute-start.3 = (bf16[16,128,128]{2,1,0:T(8,128)(2,1)}, bf16[16,128,128]{2,1,0:T(8,128)(2,1)}, u32[]{:S(2)}, u32[]{:S(2)}) collective-permute-start(bf16[16,128,128]{2,1,0:T(8,128)(2,1)} %get-tuple-element.922), channel_id=1, source_target_pairs={{4,0},{8,4},{12,8},{16,12},{20,16},{24,20},{28,24},{32,28},{36,32}... | collective-permute-start | bytes 1572872 | tf_op jit(solution)/shard_map/ppermute | solution.py:18
  (130 other events, 516.3 us)
where the time goes:
time: 1010 us; the launch traced here: 998 us
  blocking collectives  548 us (54%)
  local copies, waits for them, and re-layouts  145 us (14%)
  matrix products  97.4 us (10%)
  other arithmetic  80.2 us (8%)
  waiting for transfers between devices  66.5 us (7%)
  starting transfers between devices  40.3 us (4%)
  loops' own time  19.1 us (2%)
    psum x1, blocking collectives, shards(): temper_total = lax.psum(temper_local, ('seq', 'dp'))  87.1 us
    all_to_all x1, blocking collectives, shards(): lax.all_to_all(to_peers(query_home), 'seq', split_axis=0, concat_axis=0,...  62.3 us
    all_to_all x1, blocking collectives, shards(): lax.all_to_all(to_owner(owner_results[4]), 'seq', split_axis=0, concat_ax...  57.1 us
    all_to_all x1, blocking collectives, shards(): lax.all_to_all(to_peers(prev_keys), 'seq', split_axis=0, concat_axis=0, t...  56.9 us
    all_to_all x1, blocking collectives, shards(): lax.all_to_all(to_owner(owner_results[1]), 'seq', split_axis=0, concat_ax...  56.9 us
    all_to_all x1, blocking collectives, shards(): lax.all_to_all(to_peers(key_home), 'seq', split_axis=0, concat_axis=0, ti...  56.9 us
    all_to_all x1, blocking collectives, shards(): lax.all_to_all(to_peers(prev_values), 'seq', split_axis=0, concat_axis=0,...  56.9 us
    all_to_all x1, blocking collectives, shards(): lax.all_to_all(to_peers(grad_home), 'seq', split_axis=0, concat_axis=0, t...  56.9 us
  transfers between devices with their start and end apart: 7, of which 2 were waited for; matrix products, arithmetic and copies ran while one was open for 7% of the time, Pallas kernels for 0%

commit v1 on v0

v1 whole, which is shorter than its diff:
```python
import functools
import math

import jax
import jax.numpy as jnp
from jax import lax
from jax.experimental import pallas as pl
from jax.experimental.pallas import tpu as pltpu
from jax.sharding import PartitionSpec as P

HD = 128
BLK = 128
MOST = 12
NC = 8
HEADS = 16
Z = 8
CHIPS = 32
BLOCKS = 64
DOCS = 4
OFF = -1e30
F32 = jnp.float32
BF16 = jnp.bfloat16


def chip_of(head):
    row = head // 4
    return row * Z + 2 * (head % 4) + row % 2


def place():
    me = lax.axis_index("seq")
    chip = me // 2
    row, col = chip // Z, chip % Z
    serves = (row + col) % 2 == 0
    return me, chip, me % 2, serves, row * 4 + col // 2


def loop(count, body):
    def step(i, carry):
        body(i)
        return carry

    lax.fori_loop(0, count, step, 0)


def head_cols(head):
    return pl.ds(pl.multiple_of(head * HD, HD), HD)


def scatter_kernel(q_ref, k_ref, v_ref, g_ref, qg_ref, kv_ref, send_sem, qg_sem, kv_sem, pass_send, pass_recv):
    me, chip, core, serves, _ = place()
    partner = me + 1 - 2 * core
    barrier = pltpu.get_barrier_semaphore()

    @pl.when(serves)
    def _():
        def greet(s):
            @pl.when(s != chip)
            def _():
                pl.semaphore_signal(barrier, inc=1, device_id={"seq": 2 * s + core})

        loop(CHIPS, greet)
        pl.semaphore_signal(barrier, inc=1, device_id={"seq": partner})

    pl.semaphore_wait(barrier, HEADS)

    def pieces(head):
        cols = head_cols(head)
        return (
            (k_ref.at[0, :, cols], kv_ref.at[me, 0], kv_sem.at[chip]),
            (v_ref.at[0, :, cols], kv_ref.at[me, 1], kv_sem.at[chip]),
            (q_ref.at[0, :, cols], qg_ref.at[chip, 0], qg_sem.at[chip]),
            (g_ref.at[0, :, cols], qg_ref.at[chip, 1], qg_sem.at[chip]),
        )

    def send(turn):
        head = (turn + chip // 2) % HEADS
        target = 2 * chip_of(head) + core

        @pl.when(target != me)
        def _():
            for src, dst, sem in pieces(head):
                pltpu.make_async_remote_copy(
                    src_ref=src,
                    dst_ref=dst,
                    send_sem=send_sem.at[head],
                    recv_sem=sem,
                    device_id={"seq": target},
                ).start()

        @pl.when(target == me)
        def _():
            for src, dst, sem in pieces(head):
                pltpu.make_async_copy(src, dst, sem).start()

    loop(HEADS, send)

    def handed(s):
        block = 2 * s + core
        return pltpu.make_async_remote_copy(
            src_ref=kv_ref.at[block],
            dst_ref=kv_ref.at[block],
            send_sem=pass_send.at[s],
            recv_sem=pass_recv.at[s],
            device_id={"seq": partner},
        )

    @pl.when(serves)
    def _():
        def take(turn):
            s = (turn + chip) % CHIPS
            block = 2 * s + core
            pltpu.make_async_copy(kv_ref.at[block], kv_ref.at[block], kv_sem.at[s]).wait()
            handed(s).start()

        loop(CHIPS, take)

        def finish(s):
            other = 2 * s + 1 - core
            pltpu.make_async_copy(qg_ref.at[s], qg_ref.at[s], qg_sem.at[s]).wait()
            pltpu.make_async_copy(kv_ref.at[other], kv_ref.at[other], pass_recv.at[s]).wait()
            handed(s).wait_send()

        loop(CHIPS, finish)

    def sent(head):
        @pl.when(2 * chip_of(head) + core != me)
        def _():
            whole = kv_ref.at[pl.ds(0, 2)]
            pltpu.make_async_copy(whole, whole, send_sem.at[head]).wait()

    loop(HEADS, sent)


def scatter_blocks(q, k, v, g):
    hbm = pl.BlockSpec(memory_space=pl.ANY)
    return pl.pallas_call(
        scatter_kernel,
        out_shape=(
            jax.ShapeDtypeStruct((CHIPS, 2, BLK, HD), BF16),
            jax.ShapeDtypeStruct((BLOCKS, 2, BLK, HD), BF16),
        ),
        in_specs=[hbm] * 4,
        out_specs=(hbm, hbm),
        scratch_shapes=[
            pltpu.SemaphoreType.DMA((HEADS,)),
            pltpu.SemaphoreType.DMA((CHIPS,)),
            pltpu.SemaphoreType.DMA((CHIPS,)),
            pltpu.SemaphoreType.DMA((CHIPS,)),
            pltpu.SemaphoreType.DMA((CHIPS,)),
        ],
        compiler_params=pltpu.CompilerParams(collective_id=1, has_side_effects=True),
        name="scatter_blocks",
    )(q, k, v, g)


def dot_nt(a, b):
    return lax.dot_general(a, b, (((1,), (1,)), ((), ())), preferred_element_type=F32)


def attend_kernel(
    where_ref,
    ids_ref,
    soft_ref,
    span_ref,
    qg_ref,
    kv_hbm,
    dq_ref,
    own_ref,
    oth_ref,
    temper_ref,
    k_sc,
    v_sc,
    kt_sc,
    dk_acc,
    dv_acc,
    s_sc,
    d_sc,
    p_sc,
    e_sc,
    t_acc,
    slot_ref,
    count_ref,
    sems,
):
    core, serves, head = where_ref[0], where_ref[1], where_ref[2]
    inverse_root = 1.0 / math.sqrt(HD)
    log2e = 1.4426950408889634

    @pl.when(serves == 1)
    def _():
        temper = soft_ref[head]
        width = span_ref[head]
        scale = temper * inverse_root
        power = scale * log2e

        def clear(c):
            count_ref[c] = 0

        loop(NC, clear)

        def fetch(b):
            cluster = ids_ref[head, b]
            rank = count_ref[cluster]
            count_ref[cluster] = rank + 1
            slot = cluster * MOST + rank
            slot_ref[b] = slot
            rows = pl.ds(pl.multiple_of(slot * BLK, BLK), BLK)
            pltpu.make_async_copy(kv_hbm.at[b, 0], k_sc.at[rows], sems.at[0]).start()
            pltpu.make_async_copy(kv_hbm.at[b, 1], v_sc.at[rows], sems.at[1]).start()

        loop(BLOCKS, fetch)
        t_acc[...] = jnp.zeros_like(t_acc)

        def zero(i):
            rows = pl.ds(pl.multiple_of(i * BLK, BLK), BLK)
            dk_acc[rows, :] = jnp.zeros((BLK, HD), F32)
            dv_acc[rows, :] = jnp.zeros((BLK, HD), F32)

        loop(NC * MOST, zero)
        eye = (
            lax.broadcasted_iota(jnp.int32, (HD, HD), 0)
            == lax.broadcasted_iota(jnp.int32, (HD, HD), 1)
        ).astype(BF16)
        gap = lax.broadcasted_iota(jnp.int32, (BLK, BLK), 0) - lax.broadcasted_iota(
            jnp.int32, (BLK, BLK), 1
        )
        all_rows = pl.ds(0, BLOCKS * BLK)
        pltpu.make_async_copy(k_sc.at[all_rows], k_sc.at[all_rows], sems.at[0]).wait()
        pltpu.make_async_copy(v_sc.at[all_rows], v_sc.at[all_rows], sems.at[1]).wait()

        def blank(c):
            @pl.when(count_ref[c] % 2 == 1)
            def _():
                rows = pl.ds(pl.multiple_of((c * MOST + count_ref[c]) * BLK, BLK), BLK)
                k_sc[rows, :] = jnp.zeros((BLK, HD), BF16)
                v_sc[rows, :] = jnp.zeros((BLK, HD), BF16)
                kt_sc[:, rows] = jnp.zeros((HD, BLK), BF16)

        loop(NC, blank)

        def turn_keys(b):
            start = pl.multiple_of(slot_ref[b] * BLK, BLK)
            kt_sc[:, pl.ds(start, BLK)] = dot_nt(eye, k_sc[pl.ds(start, BLK), :]).astype(BF16)

        loop(BLOCKS, turn_keys)

        def query_block(i, block, slot, cluster, rank, blocks):
            rows = blocks * BLK
            q = qg_ref[i, 0]
            g = qg_ref[i, 1]
            first = pl.multiple_of(cluster * (MOST * BLK), BLK)
            span = pl.ds(first, rows)
            before = jnp.maximum(block - 1, 0)
            before_slot = slot_ref[before]
            usable = (block >= 1) & (before_slot // MOST != cluster)
            edge = jnp.where(usable, BLK - width, 2 * BLK)
            wstart = pl.multiple_of(before_slot * BLK, BLK)
            wspan = pl.ds(wstart, BLK)
            limit = (rank - blocks + 2) * BLK

            s_sc[pl.ds(0, rows), :] = dot_nt(k_sc[span, :], q)
            d_sc[pl.ds(0, rows), :] = dot_nt(v_sc[span, :], g)
            s_win = jnp.where(gap > edge, dot_nt(k_sc[wspan, :], q), OFF)
            s_sc[pl.ds(rows, BLK), :] = s_win
            d_sc[pl.ds(rows, BLK), :] = dot_nt(v_sc[wspan, :], g)
            for j in (blocks - 2, blocks - 1):
                part = pl.ds(j * BLK, BLK)
                shift = (j - blocks + 2) * BLK
                s_sc[part, :] = jnp.where(gap <= limit - shift, s_sc[part, :], OFF)
            top = jnp.full((8, BLK), OFF, F32)
            for j in range(blocks + 1):
                tile = s_sc[pl.ds(j * BLK, BLK), :]
                top = jnp.maximum(top, jnp.max(tile.reshape(BLK // 8, 8, BLK), axis=0))
            top = jnp.max(top, axis=0, keepdims=True)
            total = jnp.zeros((8, BLK), F32)
            mass = jnp.zeros((8, BLK), F32)
            for j in range(blocks + 1):
                part = pl.ds(j * BLK, BLK)
                weight = jnp.exp2((s_sc[part, :] - top) * power)
                p_sc[part, :] = weight
                total = total + jnp.sum(weight.reshape(BLK // 8, 8, BLK), axis=0)
                mass = mass + jnp.sum((weight * d_sc[part, :]).reshape(BLK // 8, 8, BLK), axis=0)
            inverse = 1.0 / jnp.sum(total, axis=0, keepdims=True)
            delta = jnp.sum(mass, axis=0, keepdims=True) * inverse
            terms = jnp.zeros((8, BLK), F32)
            for j in range(blocks + 1):
                part = pl.ds(j * BLK, BLK)
                prob = p_sc[part, :] * inverse
                score = prob * (d_sc[part, :] - delta)
                terms = terms + jnp.sum((score * s_sc[part, :]).reshape(BLK // 8, 8, BLK), axis=0)
                e_sc[0, part, :] = prob.astype(BF16)
                e_sc[1, part, :] = score.astype(BF16)
            t_acc[...] += terms
            body = pl.ds(0, rows)
            tail = pl.ds(rows, BLK)
            dv_acc[span, :] += jnp.dot(e_sc[0, body, :], g, preferred_element_type=F32)
            dv_acc[wspan, :] += jnp.dot(e_sc[0, tail, :], g, preferred_element_type=F32)
            dk_acc[span, :] += jnp.dot(e_sc[1, body, :], q, preferred_element_type=F32)
            dk_acc[wspan, :] += jnp.dot(e_sc[1, tail, :], q, preferred_element_type=F32)
            turned = jnp.dot(kt_sc[:, span], e_sc[1, body, :], preferred_element_type=F32)
            turned += jnp.dot(kt_sc[:, wspan], e_sc[1, tail, :], preferred_element_type=F32)
            dq_ref[i] = (turned * scale).T.astype(BF16)

        def query_step(i):
            block = 2 * i + core
            slot = slot_ref[block]
            cluster = slot // MOST
            rank = slot % MOST
            for blocks in range(2, MOST + 1, 2):

                @pl.when(rank // 2 == blocks // 2 - 1)
                def _():
                    query_block(i, block, slot, cluster, rank, blocks)

        loop(CHIPS, query_step)

        def give(i):
            mine = pl.ds(pl.multiple_of(slot_ref[2 * i + core] * BLK, BLK), BLK)
            other = pl.ds(pl.multiple_of(slot_ref[2 * i + 1 - core] * BLK, BLK), BLK)
            own_ref[i, 0] = dk_acc[mine, :] * scale
            own_ref[i, 1] = dv_acc[mine, :]
            oth_ref[i, 0] = (dk_acc[other, :] * scale).astype(BF16)
            oth_ref[i, 1] = dv_acc[other, :].astype(BF16)

        loop(CHIPS, give)
        whole = jnp.sum(jnp.sum(t_acc[...], axis=0, keepdims=True), axis=1, keepdims=True)
        temper_ref[0] = jnp.broadcast_to(whole * inverse_root, (1, BLK))


def attend(where, ids, soft, span, qg, kv):
    smem = pl.BlockSpec(memory_space=pltpu.SMEM)
    vmem = pl.BlockSpec(memory_space=pltpu.VMEM)
    slots = NC * MOST * BLK
    return pl.pallas_call(
        attend_kernel,
        out_shape=(
            jax.ShapeDtypeStruct((CHIPS, BLK, HD), BF16),
            jax.ShapeDtypeStruct((CHIPS, 2, BLK, HD), F32),
            jax.ShapeDtypeStruct((CHIPS, 2, BLK, HD), BF16),
            jax.ShapeDtypeStruct((1, 1, BLK), F32),
        ),
        in_specs=[smem, smem, smem, smem, vmem, pl.BlockSpec(memory_space=pl.ANY)],
        out_specs=(vmem, vmem, vmem, vmem),
        scratch_shapes=[
            pltpu.VMEM((slots, HD), BF16),
            pltpu.VMEM((slots, HD), BF16),
            pltpu.VMEM((HD, slots), BF16),
            pltpu.VMEM((slots, HD), F32),
            pltpu.VMEM((slots, HD), F32),
            pltpu.VMEM(((MOST + 1) * BLK, BLK), F32),
            pltpu.VMEM(((MOST + 1) * BLK, BLK), F32),
            pltpu.VMEM(((MOST + 1) * BLK, BLK), F32),
            pltpu.VMEM((2, (MOST + 1) * BLK, BLK), BF16),
            pltpu.VMEM((8, BLK), F32),
            pltpu.SMEM((BLOCKS,), jnp.int32),
            pltpu.SMEM((NC,), jnp.int32),
            pltpu.SemaphoreType.DMA((2,)),
        ],
        name="attend",
    )(where, ids, soft, span, qg, kv)


CHUNKS = 8
PER = CHIPS // CHUNKS
PEERS = DOCS * 2


def gather_kernel(
    dq_in,
    own_in,
    oth_in,
    temper_in,
    dq_ref,
    dk_ref,
    dv_ref,
    temper_ref,
    own_v,
    their_v,
    res_v,
    t_heads,
    t_all,
    own_sem,
    their_send,
    their_recv,
    home_send,
    home_recv,
    temper_send,
    temper_recv,
    peer_send,
    peer_recv,
):
    me, chip, core, serves, head = place()
    doc = lax.axis_index("dp")
    partner = me + 1 - 2 * core
    my_peer = doc * 2 + core
    barrier = pltpu.get_barrier_semaphore()

    def peer_id(j):
        return {"seq": 2 * chip + j % 2, "dp": j // 2}

    def greet_server(h):
        target = 2 * chip_of(h) + core

        @pl.when(target != me)
        def _():
            pl.semaphore_signal(barrier, inc=1, device_id={"seq": target})

    loop(HEADS, greet_server)

    def greet_peer(j):
        @pl.when(j != my_peer)
        def _():
            pl.semaphore_signal(barrier, inc=1, device_id=peer_id(j))

    loop(PEERS, greet_peer)
    pl.semaphore_wait(barrier, jnp.where(serves, CHIPS - 1 + PEERS - 1, PEERS - 1))

    def home(s, src, dst, lane, start):
        target = 2 * s + core

        @pl.when(target != me)
        def _():
            copy = pltpu.make_async_remote_copy(
                src_ref=src,
                dst_ref=dst,
                send_sem=home_send.at[lane, s],
                recv_sem=home_recv.at[lane, head],
                device_id={"seq": target},
            )
            if start:
                copy.start()
            else:
                copy.wait_send()

        if start:

            @pl.when(target == me)
            def _():
                pltpu.make_async_copy(src, dst, home_recv.at[lane, head]).start()

    def home_dq(s, start):
        home(s, dq_in.at[s], dq_ref.at[0, :, head_cols(head)], 0, start)

    def home_dk(s, start):
        home(s, res_v.at[s, 0], dk_ref.at[0, :, head_cols(head)], 1, start)

    def home_dv(s, start):
        home(s, res_v.at[s, 1], dv_ref.at[0, :, head_cols(head)], 2, start)

    def home_temper(s, start):
        target = 2 * s + core

        @pl.when(target != me)
        def _():
            copy = pltpu.make_async_remote_copy(
                src_ref=temper_in.at[0],
                dst_ref=t_heads.at[head],
                send_sem=temper_send.at[s],
                recv_sem=temper_recv.at[head],
                device_id={"seq": target},
            )
            if start:
                copy.start()
            else:
                copy.wait_send()

        if start:

            @pl.when(target == me)
            def _():
                pltpu.make_async_copy(temper_in.at[0], t_heads.at[head], temper_recv.at[head]).start()

    def theirs(j):
        part = pl.ds(j * PER, PER)
        return pltpu.make_async_remote_copy(
            src_ref=oth_in.at[part],
            dst_ref=their_v.at[part],
            send_sem=their_send.at[j],
            recv_sem=their_recv.at[j],
            device_id={"seq": partner},
        )

    def mine(j):
        part = pl.ds(j * PER, PER)
        return pltpu.make_async_copy(own_in.at[part], own_v.at[part], own_sem.at[j])

    def turned(i):
        return (i + chip) % CHIPS

    @pl.when(serves)
    def _():
        def begin(j):
            theirs(j).start()
            mine(j).start()

        loop(CHUNKS, begin)

        def send_first(i):
            s = turned(i)
            home_temper(s, True)
            home_dq(s, True)

        loop(CHIPS, send_first)

        def add(j):
            mine(j).wait()
            theirs(j).wait_recv()

            def add_one(i):
                s = j * PER + i
                res_v[s, 0] = (own_v[s, 0] + their_v[s, 0].astype(F32)).astype(BF16)
                res_v[s, 1] = (own_v[s, 1] + their_v[s, 1].astype(F32)).astype(BF16)

            loop(PER, add_one)

        loop(CHUNKS, add)

        def send_rest(i):
            s = turned(i)
            home_dk(s, True)
            home_dv(s, True)

        loop(CHIPS, send_rest)

    def heard(h):
        pltpu.make_async_copy(t_heads.at[h], t_heads.at[h], temper_recv.at[h]).wait()

    loop(HEADS, heard)

    def tell(j):
        return pltpu.make_async_remote_copy(
            src_ref=t_heads,
            dst_ref=t_all.at[my_peer],
            send_sem=peer_send.at[j],
            recv_sem=peer_recv.at[my_peer],
            device_id=peer_id(j),
        )

    def tell_peer(j):
        @pl.when(j != my_peer)
        def _():
            tell(j).start()

        @pl.when(j == my_peer)
        def _():
            pltpu.make_async_copy(t_heads, t_all.at[my_peer], peer_recv.at[my_peer]).start()

    loop(PEERS, tell_peer)

    def landed(h):
        cols = head_cols(h)
        for lane, ref in enumerate((dq_ref, dk_ref, dv_ref)):
            piece = ref.at[0, :, cols]
            pltpu.make_async_copy(piece, piece, home_recv.at[lane, h]).wait()

    loop(HEADS, landed)

    def told(j):
        pltpu.make_async_copy(t_all.at[j], t_all.at[j], peer_recv.at[j]).wait()

    loop(PEERS, told)
    total = t_all[0]
    for j in range(1, PEERS):
        total = total + t_all[j]
    temper_ref[...] = total

    def spoken(j):
        @pl.when(j != my_peer)
        def _():
            tell(j).wait_send()

    loop(PEERS, spoken)

    @pl.when(serves)
    def _():
        def close(j):
            theirs(j).wait_send()

        loop(CHUNKS, close)

        def sent(s):
            home_temper(s, False)
            home_dq(s, False)
            home_dk(s, False)
            home_dv(s, False)

        loop(CHIPS, sent)


def gather_grads(dq, own, oth, temper):
    hbm = pl.BlockSpec(memory_space=pl.ANY)
    vmem = pl.BlockSpec(memory_space=pltpu.VMEM)
    whole = jax.ShapeDtypeStruct((1, BLK, HEADS * HD), BF16)
    dma = pltpu.SemaphoreType.DMA
    return pl.pallas_call(
        gather_kernel,
        out_shape=(whole, whole, whole, jax.ShapeDtypeStruct((HEADS, 1, BLK), F32)),
        in_specs=[hbm, hbm, hbm, vmem],
        out_specs=(hbm, hbm, hbm, vmem),
        scratch_shapes=[
            pltpu.VMEM((CHIPS, 2, BLK, HD), F32),
            pltpu.VMEM((CHIPS, 2, BLK, HD), BF16),
            pltpu.VMEM((CHIPS, 2, BLK, HD), BF16),
            pltpu.VMEM((HEADS, 1, BLK), F32),
            pltpu.VMEM((PEERS, HEADS, 1, BLK), F32),
            dma((CHUNKS,)),
            dma((CHUNKS,)),
            dma((CHUNKS,)),
            dma((3, CHIPS)),
            dma((3, HEADS)),
            dma((CHIPS,)),
            dma((HEADS,)),
            dma((PEERS,)),
            dma((PEERS,)),
        ],
        compiler_params=pltpu.CompilerParams(collective_id=2, has_side_effects=True),
        name="gather_grads",
    )(dq, own, oth, temper)


def shards(q, k, v, g, softness, grouping, span):
    _, _, core, serves, head = place()
    qg, kv = scatter_blocks(q, k, v, g)
    where = jnp.stack([core, serves.astype(jnp.int32), head])
    dq, own, oth, temper = attend(where, grouping.reshape(HEADS, BLOCKS), softness, span, qg, kv)
    dq, dk, dv, temper = gather_grads(dq, own, oth, temper)
    return dq, dk, dv, temper[:, 0, 0] / (DOCS * BLOCKS * BLK)


def solution(mesh):
    tokens = P("dp", "seq", None)
    return jax.shard_map(
        shards,
        mesh=mesh,
        in_specs=(tokens, tokens, tokens, tokens, P(), P("dp", None, None, None), P()),
        out_specs=(tokens, tokens, tokens, P()),
        check_vma=False,
    )
```

time: 1010 us -> 199 us (0.20); the launches traced: 998 us -> 198 us
  blocking collectives: 548 us -> 0 us
  Pallas kernels: 0 us -> 190 us
  local copies, waits for them, and re-layouts: 145 us -> 5.64 us
  matrix products: 97.4 us -> 0 us
  other arithmetic: 80.2 us -> 2 us
  waiting for transfers between devices: 66.5 us -> 0 us
  starting transfers between devices: 40.3 us -> 0 us
  loops' own time: 19.1 us -> 0 us
    all_to_all x8 -> x0, blocking collectives: 461 us -> none  [the longest x1 62.3 us: shards(): lax.all_to_all(to_peers(query_home), 'seq', split_axis=0, concat_axis=0,...]
    pallas_call x0 -> x3, Pallas kernels: none -> 190 us  [the longest x1 78.9 us: scatter_blocks(): pl.pallas_call(scatter_kernel, out_shape=(jax.ShapeDtypeStruct((CHIPS, 2,...]
    dot_general x40 -> x0, matrix products: 97.4 us -> none  [the longest x6 23.5 us: group_step(): lax.dot_general(prob_low, grad_group, (((0,), (0,)), ((), ())), preferred...]
    psum x1 -> x0, blocking collectives: 87.1 us -> none  [shards(): temper_total = lax.psum(temper_local, ('seq', 'dp'))]
    all_to_all x3 -> x0, waiting for transfers between devices: 66.5 us -> none  [the longest x1 38 us: shards(): lax.all_to_all(to_owner(owner_results[3]), 'seq', split_axis=0, concat_ax...]
    gather x32 -> x0, local copies, waits for them, and re-layouts: 58 us -> none  [the longest x6 16.5 us: members(): return jnp.take(flat, member_pos, axis=0)]
    reduce_sum x18 -> x0, other arithmetic: 36.7 us -> none  [the longest x6 20.6 us: group_step(): temper_acc = temper_acc + jnp.sum(score_grad * raw_scores)]
    dynamic_slice x25 -> x0, local copies, waits for them, and re-layouts: 30 us -> none  [the longest x12 17.6 us: shards(): lax.map(owner_pair, (query_m, key_m, value_m, grad_m, prevk_m, prevv_m, p...]
  transfers between devices with their start and end apart: 7 -> 0, of which waited for: 2 -> 0; matrix products, arithmetic and copies ran while one was open for 7% -> 0% of each run, Pallas kernels for 0% -> 0%
where the time goes in v1:
time: 199 us; the launch traced here: 198 us
  Pallas kernels  190 us (95%)
  local copies, waits for them, and re-layouts  5.64 us (3%)
  other arithmetic  2 us (1%)
    pallas_call x1, Pallas kernels, scatter_blocks(): pl.pallas_call(scatter_kernel, out_shape=(jax.ShapeDtypeStruct((CHIPS, 2,...  78.9 us
    pallas_call x1, Pallas kernels, gather_grads(): pl.pallas_call(gather_kernel, out_shape=(whole, whole, whole, jax.ShapeDt...  63 us
    pallas_call x1, Pallas kernels, attend(): pl.pallas_call(attend_kernel, out_shape=(jax.ShapeDtypeStruct((CHIPS, BLK...  47.8 us
    unnamed x3, local copies, waits for them, and re-layouts  5.64 us

profile of v1, /device:TPU:1, one launch (start us, length us, event | category | flops | bytes accessed | tf_op | source)
XLA Modules:
  0.0 198.1 jit_solution(1224183078938664437)
XLA Ops:
  0.7 0.6 pad_add_fusion.where_ref
  1.3 78.9 %scatter_blocks.1 = (bf16[32,2,128,128]{3,2,1,0:T(8,128)(2,1)}, bf16[64,2,128,128]{3,2,1,0:T(8,128)(2,1)}) custom-call(bf16[1,128,2048]{2,1,0:T(8,128)(2,1)} %q_ref.1, bf16[1,128,2048]{2,1,0:T(8,128)(2,1)} %k_ref.1, bf16[1,128,2048]{2,1,0:T(8,128)(2,1)} %v_ref.1, bf16[1,128,2048]{2,1,0:T(8,128)(2,1)} %g_ref.1), custom_call_target="tpu_custom_call" | custom-call | tf_op jit(solution)/shard_map/scatter_blocks/pallas_call | solution.py:137
  80.2 47.8 %attend.1 = (bf16[32,128,128]{2,1,0:T(8,128)(2,1)}, f32[32,2,128,128]{3,2,1,0:T(8,128)}, bf16[32,2,128,128]{3,2,1,0:T(8,128)(2,1)}, f32[1,1,128]{2,1,0:T(1,128)}) custom-call(s32[3]{0:T(128)} %pad_add_fusion.where_ref, s32[16,64]{1,0:T(8,128)} %bitcast.4, f32[16]{0:T(128)} %soft_ref.1, s32[16]{0:T(128)} %span_ref.1, ...), custom_call_target="tpu_custom_call" | custom-call | tf_op jit(solution)/shard_map/attend/pallas_call | solution.py:335
  128.0 63.0 %gather_grads.1 = (bf16[1,128,2048]{2,1,0:T(8,128)(2,1)}, bf16[1,128,2048]{2,1,0:T(8,128)(2,1)}, bf16[1,128,2048]{2,1,0:T(8,128)(2,1)}, f32[16,1,128]{2,1,0:T(1,128)}) custom-call(bf16[32,128,128]{2,1,0:T(8,128)(2,1)} %get-tuple-element.16.dq_in, f32[32,2,128,128]{3,2,1,0:T(8,128)} %get-tuple-element.17.own_in, ...), custom_call_target="tpu_custom_call" | custom-call | tf_op jit(solution)/shard_map/gather_grads/pallas_call | solution.py:596
  191.0 1.4 multiply_reduce_fusion
  192.4 1.9 copy.14
  194.3 1.9 copy.15
  196.2 1.9 copy.16

commit v2 on v1

v2 whole, which is shorter than its diff:
```python
import math

import jax
import jax.numpy as jnp
from jax import lax
from jax.experimental import pallas as pl
from jax.experimental.pallas import tpu as pltpu
from jax.sharding import PartitionSpec as P

HD = 128
BLK = 128
MOST = 12
NC = 8
HEADS = 16
Z = 8
CHIPS = 32
BLOCKS = 64
DOCS = 4
OFF = -1e30
F32 = jnp.float32
BF16 = jnp.bfloat16


def place():
    me = lax.axis_index("seq")
    row, col = me // (2 * Z), (me // 2) % Z
    core = me % 2
    inner = ((row + 1) // 2) % 2
    partner = me + 1 - 2 * core
    neighbour = me + 2 * Z * (1 - 2 * (row % 2))
    return me, row, col, core, inner, (row // 2) * Z + col, partner, neighbour


def row_of(half, inner):
    return half * (3 - 2 * inner) + inner


def member(i, inner, core):
    return 2 * (row_of(i // Z, inner) * Z + i % Z) + core


def loop(count, body):
    def step(i, carry):
        body(i)
        return carry

    lax.fori_loop(0, count, step, 0)


def head_cols(head):
    return pl.ds(pl.multiple_of(head * HD, HD), HD)


def in_turn(turn, col, way):
    k = turn // 2
    distance = jnp.where(k % 2 == 1, 4 - (k + 1) // 2, 4 + k // 2)
    return (turn % 2) * Z + (col + way * distance + Z) % Z


def scatter_kernel(
    q_ref, k_ref, v_ref, g_ref, qg_ref, kv_ref, send_sem, qg_sem, kv_sem, near_send, near_recv, pass_send, pass_recv
):
    me, _, col, core, inner, head, partner, neighbour = place()
    barrier = pltpu.get_barrier_semaphore()

    def greet(i):
        @pl.when(i != head)
        def _():
            pl.semaphore_signal(barrier, inc=1, device_id={"seq": member(i, inner, core)})

    loop(HEADS, greet)
    pl.semaphore_signal(barrier, inc=1, device_id={"seq": partner})
    pl.semaphore_signal(barrier, inc=1, device_id={"seq": neighbour})
    pl.semaphore_wait(barrier, HEADS + 1)

    def pieces(h):
        cols = head_cols(h)
        return (
            (k_ref.at[0, :, cols], kv_ref.at[me, 0], kv_sem.at[head]),
            (v_ref.at[0, :, cols], kv_ref.at[me, 1], kv_sem.at[head]),
            (q_ref.at[0, :, cols], qg_ref.at[head, 0], qg_sem.at[head]),
            (g_ref.at[0, :, cols], qg_ref.at[head, 1], qg_sem.at[head]),
        )

    for src, dst, sem in pieces(head):
        pltpu.make_async_copy(src, dst, sem).start()

    def send(turn):
        h = in_turn(turn, col, 1)

        @pl.when(h != head)
        def _():
            for src, dst, sem in pieces(h):
                pltpu.make_async_remote_copy(
                    src_ref=src,
                    dst_ref=dst,
                    send_sem=send_sem.at[h],
                    recv_sem=sem,
                    device_id={"seq": member(h, inner, core)},
                ).start()

    loop(HEADS, send)

    def handed(block, target, send, recv):
        return pltpu.make_async_remote_copy(
            src_ref=kv_ref.at[block],
            dst_ref=kv_ref.at[block],
            send_sem=send,
            recv_sem=recv,
            device_id={"seq": target},
        )

    def to_near(s):
        return handed(member(s, inner, core), neighbour, near_send.at[s], near_recv.at[s])

    def to_partner(s):
        return handed(member(s, inner, core), partner, pass_send.at[s], pass_recv.at[s])

    def near_to_partner(s):
        return handed(member(s, 1 - inner, core), partner, pass_send.at[HEADS + s], pass_recv.at[HEADS + s])

    def arrived(block, sem):
        pltpu.make_async_copy(kv_ref.at[block], kv_ref.at[block], sem).wait()

    lag = 2

    def take(turn):
        @pl.when(turn < HEADS)
        def _():
            s = in_turn(turn, col, -1)
            arrived(member(s, inner, core), kv_sem.at[s])
            to_near(s).start()
            to_partner(s).start()

        @pl.when(turn >= lag)
        def _():
            s = in_turn(turn - lag, col, -1)
            arrived(member(s, 1 - inner, core), near_recv.at[s])
            near_to_partner(s).start()

    loop(HEADS + lag, take)

    def finish(s):
        pltpu.make_async_copy(qg_ref.at[s], qg_ref.at[s], qg_sem.at[s]).wait()
        arrived(member(s, inner, 1 - core), pass_recv.at[s])
        arrived(member(s, 1 - inner, 1 - core), pass_recv.at[HEADS + s])
        to_near(s).wait_send()
        to_partner(s).wait_send()
        near_to_partner(s).wait_send()

        @pl.when(s != head)
        def _():
            whole = kv_ref.at[pl.ds(0, 2)]
            pltpu.make_async_copy(whole, whole, send_sem.at[s]).wait()

    loop(HEADS, finish)


def scatter_blocks(q, k, v, g):
    hbm = pl.BlockSpec(memory_space=pl.ANY)
    return pl.pallas_call(
        scatter_kernel,
        out_shape=(
            jax.ShapeDtypeStruct((HEADS, 2, BLK, HD), BF16),
            jax.ShapeDtypeStruct((BLOCKS, 2, BLK, HD), BF16),
        ),
        in_specs=[hbm] * 4,
        out_specs=(hbm, hbm),
        scratch_shapes=[pltpu.SemaphoreType.DMA((HEADS,))] * 5
        + [pltpu.SemaphoreType.DMA((2 * HEADS,))] * 2,
        compiler_params=pltpu.CompilerParams(collective_id=1, has_side_effects=True),
        name="scatter_blocks",
    )(q, k, v, g)


def dot_nt(a, b):
    return lax.dot_general(a, b, (((1,), (1,)), ((), ())), preferred_element_type=F32)


def attend_kernel(
    ids_ref,
    soft_ref,
    span_ref,
    qg_ref,
    kv_hbm,
    dq_ref,
    own_ref,
    oth_ref,
    temper_ref,
    k_sc,
    v_sc,
    kt_sc,
    dk_acc,
    dv_acc,
    s_sc,
    d_sc,
    p_sc,
    e_sc,
    t_acc,
    slot_ref,
    count_ref,
    sems,
):
    _, _, _, core, inner, head, _, _ = place()
    inverse_root = 1.0 / math.sqrt(HD)
    log2e = 1.4426950408889634
    temper = soft_ref[head]
    width = span_ref[head]
    scale = temper * inverse_root
    power = scale * log2e

    def clear(c):
        count_ref[c] = 0

    loop(NC, clear)

    def fetch(b):
        cluster = ids_ref[head, b]
        rank = count_ref[cluster]
        count_ref[cluster] = rank + 1
        slot = cluster * MOST + rank
        slot_ref[b] = slot
        rows = pl.ds(pl.multiple_of(slot * BLK, BLK), BLK)
        pltpu.make_async_copy(kv_hbm.at[b, 0], k_sc.at[rows], sems.at[0]).start()
        pltpu.make_async_copy(kv_hbm.at[b, 1], v_sc.at[rows], sems.at[1]).start()

    loop(BLOCKS, fetch)
    t_acc[...] = jnp.zeros_like(t_acc)

    def zero(i):
        rows = pl.ds(pl.multiple_of(i * BLK, BLK), BLK)
        dk_acc[rows, :] = jnp.zeros((BLK, HD), F32)
        dv_acc[rows, :] = jnp.zeros((BLK, HD), F32)

    loop(NC * MOST, zero)
    eye = (
        lax.broadcasted_iota(jnp.int32, (HD, HD), 0)
        == lax.broadcasted_iota(jnp.int32, (HD, HD), 1)
    ).astype(BF16)
    gap = lax.broadcasted_iota(jnp.int32, (BLK, BLK), 0) - lax.broadcasted_iota(
        jnp.int32, (BLK, BLK), 1
    )
    all_rows = pl.ds(0, BLOCKS * BLK)
    pltpu.make_async_copy(k_sc.at[all_rows], k_sc.at[all_rows], sems.at[0]).wait()
    pltpu.make_async_copy(v_sc.at[all_rows], v_sc.at[all_rows], sems.at[1]).wait()

    def blank(c):
        @pl.when(count_ref[c] % 2 == 1)
        def _():
            rows = pl.ds(pl.multiple_of((c * MOST + count_ref[c]) * BLK, BLK), BLK)
            k_sc[rows, :] = jnp.zeros((BLK, HD), BF16)
            v_sc[rows, :] = jnp.zeros((BLK, HD), BF16)
            kt_sc[:, rows] = jnp.zeros((HD, BLK), BF16)

    loop(NC, blank)

    def turn_keys(group):
        for j in range(8):
            start = pl.multiple_of(slot_ref[group * 8 + j] * BLK, BLK)
            kt_sc[:, pl.ds(start, BLK)] = dot_nt(eye, k_sc[pl.ds(start, BLK), :]).astype(BF16)

    loop(BLOCKS // 8, turn_keys)

    def query_block(i, block, slot, cluster, rank, blocks):
        rows = blocks * BLK
        q = qg_ref[i, 0]
        g = qg_ref[i, 1]
        first = pl.multiple_of(cluster * (MOST * BLK), BLK)
        span = pl.ds(first, rows)
        before = jnp.maximum(block - 1, 0)
        before_slot = slot_ref[before]
        usable = (block >= 1) & (before_slot // MOST != cluster)
        edge = jnp.where(usable, BLK - width, 2 * BLK)
        wstart = pl.multiple_of(before_slot * BLK, BLK)
        wspan = pl.ds(wstart, BLK)
        limit = (rank - blocks + 2) * BLK

        s_sc[pl.ds(0, rows), :] = dot_nt(k_sc[span, :], q)
        d_sc[pl.ds(0, rows), :] = dot_nt(v_sc[span, :], g)
        s_win = jnp.where(gap > edge, dot_nt(k_sc[wspan, :], q), OFF)
        s_sc[pl.ds(rows, BLK), :] = s_win
        d_sc[pl.ds(rows, BLK), :] = dot_nt(v_sc[wspan, :], g)
        for j in (blocks - 2, blocks - 1):
            part = pl.ds(j * BLK, BLK)
            shift = (j - blocks + 2) * BLK
            s_sc[part, :] = jnp.where(gap <= limit - shift, s_sc[part, :], OFF)
        top = jnp.full((8, BLK), OFF, F32)
        for j in range(blocks + 1):
            tile = s_sc[pl.ds(j * BLK, BLK), :]
            top = jnp.maximum(top, jnp.max(tile.reshape(BLK // 8, 8, BLK), axis=0))
        top = jnp.max(top, axis=0, keepdims=True)
        total = jnp.zeros((8, BLK), F32)
        mass = jnp.zeros((8, BLK), F32)
        for j in range(blocks + 1):
            part = pl.ds(j * BLK, BLK)
            weight = jnp.exp2((s_sc[part, :] - top) * power)
            p_sc[part, :] = weight
            total = total + jnp.sum(weight.reshape(BLK // 8, 8, BLK), axis=0)
            mass = mass + jnp.sum((weight * d_sc[part, :]).reshape(BLK // 8, 8, BLK), axis=0)
        inverse = 1.0 / jnp.sum(total, axis=0, keepdims=True)
        delta = jnp.sum(mass, axis=0, keepdims=True) * inverse
        terms = jnp.zeros((8, BLK), F32)
        for j in range(blocks + 1):
            part = pl.ds(j * BLK, BLK)
            prob = p_sc[part, :] * inverse
            score = prob * (d_sc[part, :] - delta)
            terms = terms + jnp.sum((score * s_sc[part, :]).reshape(BLK // 8, 8, BLK), axis=0)
            e_sc[0, part, :] = prob.astype(BF16)
            e_sc[1, part, :] = score.astype(BF16)
        t_acc[...] += terms
        body = pl.ds(0, rows)
        tail = pl.ds(rows, BLK)
        dv_acc[span, :] += jnp.dot(e_sc[0, body, :], g, preferred_element_type=F32)
        dv_acc[wspan, :] += jnp.dot(e_sc[0, tail, :], g, preferred_element_type=F32)
        dk_acc[span, :] += jnp.dot(e_sc[1, body, :], q, preferred_element_type=F32)
        dk_acc[wspan, :] += jnp.dot(e_sc[1, tail, :], q, preferred_element_type=F32)
        turned = jnp.dot(kt_sc[:, span], e_sc[1, body, :], preferred_element_type=F32)
        turned += jnp.dot(kt_sc[:, wspan], e_sc[1, tail, :], preferred_element_type=F32)
        dq_ref[i] = (turned * scale).T.astype(BF16)

    def query_step(i):
        block = member(i, inner, core)
        slot = slot_ref[block]
        cluster = slot // MOST
        rank = slot % MOST
        for blocks in range(2, MOST + 1, 2):

            @pl.when(rank // 2 == blocks // 2 - 1)
            def _():
                query_block(i, block, slot, cluster, rank, blocks)

    loop(HEADS, query_step)

    def give(i):
        mine = pl.ds(pl.multiple_of(slot_ref[2 * i + core] * BLK, BLK), BLK)
        other = pl.ds(pl.multiple_of(slot_ref[2 * i + 1 - core] * BLK, BLK), BLK)
        own_ref[i, 0] = dk_acc[mine, :] * scale
        own_ref[i, 1] = dv_acc[mine, :]
        oth_ref[i, 0] = (dk_acc[other, :] * scale).astype(BF16)
        oth_ref[i, 1] = dv_acc[other, :].astype(BF16)

    loop(CHIPS, give)
    whole = jnp.sum(jnp.sum(t_acc[...], axis=0, keepdims=True), axis=1, keepdims=True)
    temper_ref[0] = jnp.broadcast_to(whole * inverse_root, (1, BLK))


def attend(ids, soft, span, qg, kv):
    smem = pl.BlockSpec(memory_space=pltpu.SMEM)
    vmem = pl.BlockSpec(memory_space=pltpu.VMEM)
    slots = NC * MOST * BLK
    return pl.pallas_call(
        attend_kernel,
        out_shape=(
            jax.ShapeDtypeStruct((HEADS, BLK, HD), BF16),
            jax.ShapeDtypeStruct((CHIPS, 2, BLK, HD), F32),
            jax.ShapeDtypeStruct((CHIPS, 2, BLK, HD), BF16),
            jax.ShapeDtypeStruct((1, 1, BLK), F32),
        ),
        in_specs=[smem, smem, smem, vmem, pl.BlockSpec(memory_space=pl.ANY)],
        out_specs=(vmem, vmem, vmem, vmem),
        scratch_shapes=[
            pltpu.VMEM((slots, HD), BF16),
            pltpu.VMEM((slots, HD), BF16),
            pltpu.VMEM((HD, slots), BF16),
            pltpu.VMEM((slots, HD), F32),
            pltpu.VMEM((slots, HD), F32),
            pltpu.VMEM(((MOST + 1) * BLK, BLK), F32),
            pltpu.VMEM(((MOST + 1) * BLK, BLK), F32),
            pltpu.VMEM(((MOST + 1) * BLK, BLK), F32),
            pltpu.VMEM((2, (MOST + 1) * BLK, BLK), BF16),
            pltpu.VMEM((8, BLK), F32),
            pltpu.SMEM((BLOCKS,), jnp.int32),
            pltpu.SMEM((NC,), jnp.int32),
            pltpu.SemaphoreType.DMA((2,)),
        ],
        name="attend",
    )(ids, soft, span, qg, kv)


CHUNKS = 8
PER = CHIPS // CHUNKS
HALF = CHUNKS // 2
PEERS = DOCS * 4


def chunk_of(u, inner):
    return 2 * row_of(u // 2, inner) + u % 2


def gather_kernel(
    dq_in,
    own_in,
    oth_in,
    temper_in,
    dq_ref,
    dk_ref,
    dv_ref,
    temper_ref,
    own_v,
    their_v,
    give_v,
    near_v,
    res_v,
    t_heads,
    t_all,
    own_sem,
    their_send,
    their_recv,
    near_send,
    near_recv,
    home_send,
    home_recv,
    temper_send,
    temper_recv,
    peer_send,
    peer_recv,
):
    me, row, col, core, inner, head, partner, neighbour = place()
    doc = lax.axis_index("dp")
    my_peer = doc * 4 + inner * 2 + core
    barrier = pltpu.get_barrier_semaphore()

    def peer_id(j):
        half = row // 2
        other = 2 * half + ((j // 2) % 2 + half) % 2
        return {"seq": 2 * (other * Z + col) + j % 2, "dp": j // 4}

    def greet_member(i):
        @pl.when(i != head)
        def _():
            pl.semaphore_signal(barrier, inc=1, device_id={"seq": member(i, inner, core)})

    loop(HEADS, greet_member)

    def greet_peer(j):
        @pl.when(j != my_peer)
        def _():
            pl.semaphore_signal(barrier, inc=1, device_id=peer_id(j))

    loop(PEERS, greet_peer)
    pl.semaphore_wait(barrier, HEADS - 1 + PEERS - 1)

    def home_copy(i, src, dst, lane):
        return pltpu.make_async_remote_copy(
            src_ref=src,
            dst_ref=dst.at[0, :, head_cols(head)],
            send_sem=home_send.at[lane, i],
            recv_sem=home_recv.at[lane, head],
            device_id={"seq": member(i, inner, core)},
        )

    def lanes(i):
        return (
            (dq_in.at[i], dq_ref, 0),
            (res_v.at[i, 0], dk_ref, 1),
            (res_v.at[i, 1], dv_ref, 2),
        )

    def go_home(i, src, dst, lane):
        @pl.when(i != head)
        def _():
            home_copy(i, src, dst, lane).start()

        @pl.when(i == head)
        def _():
            pltpu.make_async_copy(src, dst.at[0, :, head_cols(head)], home_recv.at[lane, head]).start()

    def temper_copy(i):
        return pltpu.make_async_remote_copy(
            src_ref=temper_in.at[0],
            dst_ref=t_heads.at[head],
            send_sem=temper_send.at[i],
            recv_sem=temper_recv.at[head],
            device_id={"seq": member(i, inner, core)},
        )

    def theirs(j):
        part = pl.ds(j * PER, PER)
        return pltpu.make_async_remote_copy(
            src_ref=oth_in.at[part],
            dst_ref=their_v.at[part],
            send_sem=their_send.at[j],
            recv_sem=their_recv.at[j],
            device_id={"seq": partner},
        )

    def mine(j):
        part = pl.ds(j * PER, PER)
        return pltpu.make_async_copy(own_in.at[part], own_v.at[part], own_sem.at[j])

    def near(u):
        part = pl.ds(u * PER, PER)
        return pltpu.make_async_remote_copy(
            src_ref=give_v.at[part],
            dst_ref=near_v.at[part],
            send_sem=near_send.at[u],
            recv_sem=near_recv.at[u],
            device_id={"seq": neighbour},
        )

    def chunk_in_order(step):
        return jnp.where(step < HALF, chunk_of(step % HALF, 1 - inner), chunk_of(step % HALF, inner))

    def begin(step):
        j = chunk_in_order(step)
        theirs(j).start()
        mine(j).start()

    loop(CHUNKS, begin)
    pltpu.make_async_copy(temper_in.at[0], t_heads.at[head], temper_recv.at[head]).start()

    def send_first(turn):
        i = in_turn(turn, col, 1)

        @pl.when(i != head)
        def _():
            temper_copy(i).start()

        go_home(i, *lanes(i)[0])

    loop(HEADS, send_first)

    def give(u):
        @pl.when(u < HALF)
        def _():
            j = chunk_of(u, 1 - inner)
            mine(j).wait()
            theirs(j).wait_recv()

            def add_one(i):
                for x in (0, 1):
                    total = own_v[j * PER + i, x] + their_v[j * PER + i, x].astype(F32)
                    give_v[u * PER + i, x] = total.astype(BF16)

            loop(PER, add_one)

        @pl.when(u > 0)
        def _():
            near(u - 1).start()

    loop(HALF + 1, give)

    def keep(u):
        @pl.when(u < HALF)
        def _():
            j = chunk_of(u, inner)
            mine(j).wait()
            theirs(j).wait_recv()
            near(u).wait_recv()

            def add_one(i):
                for x in (0, 1):
                    total = own_v[j * PER + i, x] + their_v[j * PER + i, x].astype(F32)
                    res_v[u * PER + i, x] = (total + near_v[u * PER + i, x].astype(F32)).astype(BF16)

            loop(PER, add_one)

        @pl.when(u > 0)
        def _():
            def send_one(i):
                s = (u - 1) * PER + i
                go_home(s, *lanes(s)[1])
                go_home(s, *lanes(s)[2])

            loop(PER, send_one)

    loop(HALF + 1, keep)

    def heard(h):
        pltpu.make_async_copy(t_heads.at[h], t_heads.at[h], temper_recv.at[h]).wait()

    loop(HEADS, heard)

    def tell(j):
        return pltpu.make_async_remote_copy(
            src_ref=t_heads,
            dst_ref=t_all.at[my_peer],
            send_sem=peer_send.at[j],
            recv_sem=peer_recv.at[my_peer],
            device_id=peer_id(j),
        )

    pltpu.make_async_copy(t_heads, t_all.at[my_peer], peer_recv.at[my_peer]).start()

    def tell_peer(j):
        @pl.when(j != my_peer)
        def _():
            tell(j).start()

    loop(PEERS, tell_peer)

    def landed(h):
        cols = head_cols(h)
        for lane, ref in enumerate((dq_ref, dk_ref, dv_ref)):
            piece = ref.at[0, :, cols]
            pltpu.make_async_copy(piece, piece, home_recv.at[lane, h]).wait()

    loop(HEADS, landed)

    def told(j):
        pltpu.make_async_copy(t_all.at[j], t_all.at[j], peer_recv.at[j]).wait()

    loop(PEERS, told)
    total = t_all[0]
    for j in range(1, PEERS):
        total = total + t_all[j]
    temper_ref[...] = total * (1.0 / (DOCS * BLOCKS * BLK))

    def sent(i):
        @pl.when(i != my_peer)
        def _():
            tell(i).wait_send()

        @pl.when(i != head)
        def _():
            temper_copy(i).wait_send()
            for lane in lanes(i):
                home_copy(i, *lane).wait_send()

    loop(HEADS, sent)

    def close(j):
        theirs(j).wait_send()

    loop(CHUNKS, close)

    def close_near(u):
        near(u).wait_send()

    loop(HALF, close_near)


def gather_grads(dq, own, oth, temper):
    hbm = pl.BlockSpec(memory_space=pl.ANY)
    vmem = pl.BlockSpec(memory_space=pltpu.VMEM)
    whole = jax.ShapeDtypeStruct((1, BLK, HEADS * HD), BF16)
    dma = pltpu.SemaphoreType.DMA
    return pl.pallas_call(
        gather_kernel,
        out_shape=(whole, whole, whole, jax.ShapeDtypeStruct((HEADS, 1, BLK), F32)),
        in_specs=[hbm, hbm, hbm, vmem],
        out_specs=(hbm, hbm, hbm, vmem),
        scratch_shapes=[
            pltpu.VMEM((CHIPS, 2, BLK, HD), F32),
            pltpu.VMEM((CHIPS, 2, BLK, HD), BF16),
            pltpu.VMEM((HEADS, 2, BLK, HD), BF16),
            pltpu.VMEM((HEADS, 2, BLK, HD), BF16),
            pltpu.VMEM((HEADS, 2, BLK, HD), BF16),
            pltpu.VMEM((HEADS, 1, BLK), F32),
            pltpu.VMEM((PEERS, HEADS, 1, BLK), F32),
            dma((CHUNKS,)),
            dma((CHUNKS,)),
            dma((CHUNKS,)),
            dma((HALF,)),
            dma((HALF,)),
            dma((3, HEADS)),
            dma((3, HEADS)),
            dma((HEADS,)),
            dma((HEADS,)),
            dma((PEERS,)),
            dma((PEERS,)),
        ],
        compiler_params=pltpu.CompilerParams(collective_id=2, has_side_effects=True),
        name="gather_grads",
    )(dq, own, oth, temper)


def settle_kernel(dq_in, dk_in, dv_in, temper_in, dq_ref, dk_ref, dv_ref, temper_ref):
    dq_ref[...] = dq_in[...]
    dk_ref[...] = dk_in[...]
    dv_ref[...] = dv_in[...]

    @pl.when(pl.program_id(0) == 0)
    def _():
        for h in range(HEADS):
            temper_ref[h] = temper_in[h, 0, 0]


def settle(dq, dk, dv, temper):
    steps = 4
    part = pl.BlockSpec((1, BLK // steps, HEADS * HD), lambda i: (0, i, 0))
    whole = jax.ShapeDtypeStruct((1, BLK, HEADS * HD), BF16)
    return pl.pallas_call(
        settle_kernel,
        grid=(steps,),
        out_shape=(whole, whole, whole, jax.ShapeDtypeStruct((HEADS,), F32)),
        in_specs=[part, part, part, pl.BlockSpec(memory_space=pltpu.VMEM)],
        out_specs=(part, part, part, pl.BlockSpec(memory_space=pltpu.SMEM)),
        name="settle",
    )(dq, dk, dv, temper)


def shards(q, k, v, g, softness, grouping, span):
    qg, kv = scatter_blocks(q, k, v, g)
    dq, own, oth, temper = attend(grouping.reshape(HEADS, BLOCKS), softness, span, qg, kv)
    return settle(*gather_grads(dq, own, oth, temper))


def solution(mesh):
    tokens = P("dp", "seq", None)
    return jax.shard_map(
        shards,
        mesh=mesh,
        in_specs=(tokens, tokens, tokens, tokens, P(), P("dp", None, None, None), P()),
        out_specs=(tokens, tokens, tokens, P()),
        check_vma=False,
    )
```

time: 199 us -> 154 us (0.77)
  the two profiles are of different devices: /device:TPU:1 before, /device:TPU:11 now
where the time goes in v2:
time: 154 us; the launch traced here: 152 us
  Pallas kernels  151 us (98%)
    pallas_call x1, Pallas kernels, scatter_blocks(): pl.pallas_call(scatter_kernel, out_shape=(jax.ShapeDtypeStruct((HEADS, 2,...  65.2 us
    pallas_call x1, Pallas kernels, gather_grads(): pl.pallas_call(gather_kernel, out_shape=(whole, whole, whole, jax.ShapeDt...  56.3 us
    pallas_call x1, Pallas kernels, attend(): pl.pallas_call(attend_kernel, out_shape=(jax.ShapeDtypeStruct((HEADS, BLK...  26.1 us
    pallas_call x1, Pallas kernels, settle(): pl.pallas_call(settle_kernel, grid=(steps,), out_shape=(whole, whole, who...  3.67 us

profile of v2, /device:TPU:11, one launch (start us, length us, event | category | flops | bytes accessed | tf_op | source)
XLA Modules:
  0.0 151.9 jit_solution(2471432848265569819)
XLA Ops:
  0.6 65.2 %scatter_blocks.1 = (bf16[16,2,128,128]{3,2,1,0:T(8,128)(2,1)}, bf16[64,2,128,128]{3,2,1,0:T(8,128)(2,1)}) custom-call(bf16[1,128,2048]{2,1,0:T(8,128)(2,1)} %q_ref.1, bf16[1,128,2048]{2,1,0:T(8,128)(2,1)} %k_ref.1, bf16[1,128,2048]{2,1,0:T(8,128)(2,1)} %v_ref.1, bf16[1,128,2048]{2,1,0:T(8,128)(2,1)} %g_ref.1), custom_call_target="tpu_custom_call" | custom-call | tf_op jit(solution)/shard_map/scatter_blocks/pallas_call | solution.py:161
  65.9 26.1 %attend.1 = (bf16[16,128,128]{2,1,0:T(8,128)(2,1)}, f32[32,2,128,128]{3,2,1,0:T(8,128)}, bf16[32,2,128,128]{3,2,1,0:T(8,128)(2,1)}, f32[1,1,128]{2,1,0:T(1,128)}) custom-call(s32[16,64]{1,0:T(8,128)} %bitcast.1, f32[16]{0:T(128)} %soft_ref.1, s32[16]{0:T(128)} %span_ref.1, bf16[16,2,128,128]{3,2,1,0:T(8,128)(2,1)} %get-tuple-element.14.qg_ref, ...), custom_call_target="tpu_custom_call" | custom-call | tf_op jit(solution)/shard_map/attend/pallas_call | solution.py:351
  91.9 56.3 %gather_grads.1 = (bf16[1,128,2048]{2,1,0:T(8,128)(2,1)}, bf16[1,128,2048]{2,1,0:T(8,128)(2,1)}, bf16[1,128,2048]{2,1,0:T(8,128)(2,1)}, f32[16,1,128]{2,1,0:T(1,128)}) custom-call(bf16[16,128,128]{2,1,0:T(8,128)(2,1)} %get-tuple-element.16.dq_in, f32[32,2,128,128]{3,2,1,0:T(8,128)} %get-tuple-element.17.own_in, ...), custom_call_target="tpu_custom_call" | custom-call | tf_op jit(solution)/shard_map/gather_grads/pallas_call | solution.py:638
  148.3 3.7 %settle.1 = (bf16[1,128,2048]{2,1,0:T(8,128)(2,1)}, bf16[1,128,2048]{2,1,0:T(8,128)(2,1)}, bf16[1,128,2048]{2,1,0:T(8,128)(2,1)}, f32[16]{0:T(128)}) custom-call(bf16[1,128,2048]{2,1,0:T(8,128)(2,1)} %get-tuple-element.20.dq_in, bf16[1,128,2048]{2,1,0:T(8,128)(2,1)} %get-tuple-element.21.dk_in, bf16[1,128,2048]{2,1,0:T(8,128)(2,1)} %get-tuple-element.22.dv_in, ...), custom_call_target="tpu_custom_call" | custom-call | tf_op jit(solution)/shard_map/settle/pallas_call | solution.py:683

commit v3 on v2

--- a/solution.py
+++ b/solution.py
@@ -53,8 +53,12 @@
 
 def in_turn(turn, col, way):
     k = turn // 2
-    distance = jnp.where(k % 2 == 1, 4 - (k + 1) // 2, 4 + k // 2)
+    distance = jnp.where(k == 0, 0, jnp.where(k == 7, 4, jnp.where(k % 2 == 1, (k + 1) // 2, Z - k // 2)))
     return (turn % 2) * Z + (col + way * distance + Z) % Z
+
+
+def out_turn(turn, col):
+    return in_turn(HEADS - 1 - turn, col, 1)
 
 
 def scatter_kernel(
@@ -85,21 +89,24 @@
     for src, dst, sem in pieces(head):
         pltpu.make_async_copy(src, dst, sem).start()
 
-    def send(turn):
-        h = in_turn(turn, col, 1)
-
-        @pl.when(h != head)
-        def _():
-            for src, dst, sem in pieces(h):
-                pltpu.make_async_remote_copy(
-                    src_ref=src,
-                    dst_ref=dst,
-                    send_sem=send_sem.at[h],
-                    recv_sem=sem,
-                    device_id={"seq": member(h, inner, core)},
-                ).start()
-
-    loop(HEADS, send)
+    def send(group, kinds):
+        for kind in kinds:
+            for j in (0, 2, 1, 3):
+                h = in_turn(group * 4 + j, col, 1)
+
+                @pl.when(h != head)
+                def _():
+                    src, dst, sem = pieces(h)[kind]
+                    pltpu.make_async_remote_copy(
+                        src_ref=src,
+                        dst_ref=dst,
+                        send_sem=send_sem.at[h],
+                        recv_sem=sem,
+                        device_id={"seq": member(h, inner, core)},
+                    ).start()
+
+    loop(HEADS // 4, lambda group: send(group, (0, 1)))
+    loop(HEADS // 4, lambda group: send(group, (2, 3)))
 
     def handed(block, target, send, recv):
         return pltpu.make_async_remote_copy(
@@ -201,7 +208,7 @@
     count_ref,
     sems,
 ):
-    _, _, _, core, inner, head, _, _ = place()
+    _, _, col, core, inner, head, _, _ = place()
     inverse_root = 1.0 / math.sqrt(HD)
     log2e = 1.4426950408889634
     temper = soft_ref[head]
@@ -332,8 +339,10 @@
     loop(HEADS, query_step)
 
     def give(i):
-        mine = pl.ds(pl.multiple_of(slot_ref[2 * i + core] * BLK, BLK), BLK)
-        other = pl.ds(pl.multiple_of(slot_ref[2 * i + 1 - core] * BLK, BLK), BLK)
+        at = out_turn(i % HEADS, col)
+        owner = jnp.where(i < HEADS, 1 - inner, inner)
+        mine = pl.ds(pl.multiple_of(slot_ref[member(at, owner, core)] * BLK, BLK), BLK)
+        other = pl.ds(pl.multiple_of(slot_ref[member(at, owner, 1 - core)] * BLK, BLK), BLK)
         own_ref[i, 0] = dk_acc[mine, :] * scale
         own_ref[i, 1] = dv_acc[mine, :]
         oth_ref[i, 0] = (dk_acc[other, :] * scale).astype(BF16)
@@ -381,10 +390,6 @@
 PER = CHIPS // CHUNKS
 HALF = CHUNKS // 2
 PEERS = DOCS * 4
-
-
-def chunk_of(u, inner):
-    return 2 * row_of(u // 2, inner) + u % 2
 
 
 def gather_kernel(
@@ -449,13 +454,6 @@
             device_id={"seq": member(i, inner, core)},
         )
 
-    def lanes(i):
-        return (
-            (dq_in.at[i], dq_ref, 0),
-            (res_v.at[i, 0], dk_ref, 1),
-            (res_v.at[i, 1], dv_ref, 2),
-        )
-
     def go_home(i, src, dst, lane):
         @pl.when(i != head)
         def _():
@@ -498,38 +496,34 @@
             device_id={"seq": neighbour},
         )
 
-    def chunk_in_order(step):
-        return jnp.where(step < HALF, chunk_of(step % HALF, 1 - inner), chunk_of(step % HALF, inner))
-
-    def begin(step):
-        j = chunk_in_order(step)
+    def begin(j):
         theirs(j).start()
         mine(j).start()
 
     loop(CHUNKS, begin)
     pltpu.make_async_copy(temper_in.at[0], t_heads.at[head], temper_recv.at[head]).start()
 
-    def send_first(turn):
-        i = in_turn(turn, col, 1)
-
-        @pl.when(i != head)
-        def _():
-            temper_copy(i).start()
-
-        go_home(i, *lanes(i)[0])
-
-    loop(HEADS, send_first)
+    def send_first(group):
+        for j in (0, 2, 1, 3):
+            i = out_turn(group * 4 + j, col)
+
+            @pl.when(i != head)
+            def _():
+                temper_copy(i).start()
+
+            go_home(i, dq_in.at[i], dq_ref, 0)
+
+    loop(HEADS // 4, send_first)
 
     def give(u):
         @pl.when(u < HALF)
         def _():
-            j = chunk_of(u, 1 - inner)
-            mine(j).wait()
-            theirs(j).wait_recv()
+            mine(u).wait()
+            theirs(u).wait_recv()
 
             def add_one(i):
                 for x in (0, 1):
-                    total = own_v[j * PER + i, x] + their_v[j * PER + i, x].astype(F32)
+                    total = own_v[u * PER + i, x] + their_v[u * PER + i, x].astype(F32)
                     give_v[u * PER + i, x] = total.astype(BF16)
 
             loop(PER, add_one)
@@ -543,26 +537,24 @@
     def keep(u):
         @pl.when(u < HALF)
         def _():
-            j = chunk_of(u, inner)
-            mine(j).wait()
-            theirs(j).wait_recv()
+            mine(HALF + u).wait()
+            theirs(HALF + u).wait_recv()
             near(u).wait_recv()
 
             def add_one(i):
                 for x in (0, 1):
-                    total = own_v[j * PER + i, x] + their_v[j * PER + i, x].astype(F32)
+                    at = (HALF + u) * PER + i
+                    total = own_v[at, x] + their_v[at, x].astype(F32)
                     res_v[u * PER + i, x] = (total + near_v[u * PER + i, x].astype(F32)).astype(BF16)
 
             loop(PER, add_one)
 
         @pl.when(u > 0)
         def _():
-            def send_one(i):
-                s = (u - 1) * PER + i
-                go_home(s, *lanes(s)[1])
-                go_home(s, *lanes(s)[2])
-
-            loop(PER, send_one)
+            for x in (0, 1):
+                for j in (0, 2, 1, 3):
+                    t = (u - 1) * PER + j
+                    go_home(out_turn(t, col), res_v.at[t, x], (dk_ref, dv_ref)[x], 1 + x)
 
     loop(HALF + 1, keep)
 
@@ -589,6 +581,18 @@
 
     loop(PEERS, tell_peer)
 
+    def told(j):
+        pltpu.make_async_copy(t_all.at[j], t_all.at[j], peer_recv.at[j]).wait()
+
+    loop(PEERS, told)
+    total = t_all[0]
+    for j in range(1, PEERS):
+        total = total + t_all[j]
+    total = total * (1.0 / (DOCS * BLOCKS * BLK))
+    for h in range(HEADS):
+        temper_ref[h] = total[h, 0, 0]
+
+
     def landed(h):
         cols = head_cols(h)
         for lane, ref in enumerate((dq_ref, dk_ref, dv_ref)):
@@ -597,15 +601,6 @@
 
     loop(HEADS, landed)
 
-    def told(j):
-        pltpu.make_async_copy(t_all.at[j], t_all.at[j], peer_recv.at[j]).wait()
-
-    loop(PEERS, told)
-    total = t_all[0]
-    for j in range(1, PEERS):
-        total = total + t_all[j]
-    temper_ref[...] = total * (1.0 / (DOCS * BLOCKS * BLK))
-
     def sent(i):
         @pl.when(i != my_peer)
         def _():
@@ -614,8 +609,8 @@
         @pl.when(i != head)
         def _():
             temper_copy(i).wait_send()
-            for lane in lanes(i):
-                home_copy(i, *lane).wait_send()
+            for lane, dst in enumerate((dq_ref, dk_ref, dv_ref)):
+                home_copy(i, dq_in.at[i], dst, lane).wait_send()
 
     loop(HEADS, sent)
 
@@ -637,9 +632,9 @@
     dma = pltpu.SemaphoreType.DMA
     return pl.pallas_call(
         gather_kernel,
-        out_shape=(whole, whole, whole, jax.ShapeDtypeStruct((HEADS, 1, BLK), F32)),
+        out_shape=(whole, whole, whole, jax.ShapeDtypeStruct((HEADS,), F32)),
         in_specs=[hbm, hbm, hbm, vmem],
-        out_specs=(hbm, hbm, hbm, vmem),
+        out_specs=(hbm, hbm, hbm, pl.BlockSpec(memory_space=pltpu.SMEM)),
         scratch_shapes=[
             pltpu.VMEM((CHIPS, 2, BLK, HD), F32),
             pltpu.VMEM((CHIPS, 2, BLK, HD), BF16),
@@ -665,27 +660,47 @@
     )(dq, own, oth, temper)
 
 
-def settle_kernel(dq_in, dk_in, dv_in, temper_in, dq_ref, dk_ref, dv_ref, temper_ref):
-    dq_ref[...] = dq_in[...]
-    dk_ref[...] = dk_in[...]
-    dv_ref[...] = dv_in[...]
-
-    @pl.when(pl.program_id(0) == 0)
-    def _():
-        for h in range(HEADS):
-            temper_ref[h] = temper_in[h, 0, 0]
+PARTS = 2
+
+
+def settle_kernel(dq_in, dk_in, dv_in, temper_in, dq_ref, dk_ref, dv_ref, temper_ref, hold, in_sem, out_sem):
+    rows = BLK // PARTS
+    pairs = ((dq_in, dq_ref), (dk_in, dk_ref), (dv_in, dv_ref))
+
+    def take(n):
+        part = pl.ds((n % PARTS) * rows, rows)
+        return pltpu.make_async_copy(pairs[n // PARTS][0].at[0, part], hold.at[n], in_sem.at[n])
+
+    def put(n):
+        part = pl.ds((n % PARTS) * rows, rows)
+        return pltpu.make_async_copy(hold.at[n], pairs[n // PARTS][1].at[0, part], out_sem.at[n])
+
+    count = 3 * PARTS
+    for n in range(count):
+        take(n).start()
+    temper_copy = pltpu.make_async_copy(temper_in, temper_ref, in_sem.at[count])
+    temper_copy.start()
+    for n in range(count):
+        take(n).wait()
+        put(n).start()
+    for n in range(count):
+        put(n).wait()
+    temper_copy.wait()
 
 
 def settle(dq, dk, dv, temper):
-    steps = 4
-    part = pl.BlockSpec((1, BLK // steps, HEADS * HD), lambda i: (0, i, 0))
+    hbm = pl.BlockSpec(memory_space=pl.ANY)
     whole = jax.ShapeDtypeStruct((1, BLK, HEADS * HD), BF16)
     return pl.pallas_call(
         settle_kernel,
-        grid=(steps,),
         out_shape=(whole, whole, whole, jax.ShapeDtypeStruct((HEADS,), F32)),
-        in_specs=[part, part, part, pl.BlockSpec(memory_space=pltpu.VMEM)],
-        out_specs=(part, part, part, pl.BlockSpec(memory_space=pltpu.SMEM)),
+        in_specs=[hbm] * 4,
+        out_specs=(hbm,) * 4,
+        scratch_shapes=[
+            pltpu.VMEM((3 * PARTS, BLK // PARTS, HEADS * HD), BF16),
+            pltpu.SemaphoreType.DMA((3 * PARTS + 1,)),
+            pltpu.SemaphoreType.DMA((3 * PARTS,)),
+        ],
         name="settle",
     )(dq, dk, dv, temper)
 

time: 154 us -> 140 us (0.909)
  the two profiles are of different devices: /device:TPU:11 before, /device:TPU:1 now
where the time goes in v3:
time: 140 us
  Pallas kernels  139 us (99%)
    pallas_call x1, Pallas kernels, gather_grads(): pl.pallas_call(gather_kernel, out_shape=(whole, whole, whole, jax.ShapeDt...  56.4 us
    pallas_call x1, Pallas kernels, scatter_blocks(): pl.pallas_call(scatter_kernel, out_shape=(jax.ShapeDtypeStruct((HEADS, 2,...  54.1 us
    pallas_call x1, Pallas kernels, attend(): pl.pallas_call(attend_kernel, out_shape=(jax.ShapeDtypeStruct((HEADS, BLK...  26.5 us

profile of v3, /device:TPU:1, one launch (start us, length us, event | category | flops | bytes accessed | tf_op | source)
XLA Modules:
  0.0 139.9 jit_solution(17402922153921280866)
XLA Ops:
  0.6 54.1 %scatter_blocks.1 = (bf16[16,2,128,128]{3,2,1,0:T(8,128)(2,1)}, bf16[64,2,128,128]{3,2,1,0:T(8,128)(2,1)}) custom-call(bf16[1,128,2048]{2,1,0:T(8,128)(2,1)} %q_ref.1, bf16[1,128,2048]{2,1,0:T(8,128)(2,1)} %k_ref.1, bf16[1,128,2048]{2,1,0:T(8,128)(2,1)} %v_ref.1, bf16[1,128,2048]{2,1,0:T(8,128)(2,1)} %g_ref.1), custom_call_target="tpu_custom_call" | custom-call | tf_op jit(solution)/shard_map/scatter_blocks/pallas_call | solution.py:168
  54.8 26.5 %attend.1 = (bf16[16,128,128]{2,1,0:T(8,128)(2,1)}, f32[32,2,128,128]{3,2,1,0:T(8,128)}, bf16[32,2,128,128]{3,2,1,0:T(8,128)(2,1)}, f32[1,1,128]{2,1,0:T(1,128)}) custom-call(s32[16,64]{1,0:T(8,128)} %bitcast.1, f32[16]{0:T(128)} %soft_ref.1, s32[16]{0:T(128)} %span_ref.1, bf16[16,2,128,128]{3,2,1,0:T(8,128)(2,1)} %get-tuple-element.14.qg_ref, ...), custom_call_target="tpu_custom_call" | custom-call | tf_op jit(solution)/shard_map/attend/pallas_call | solution.py:360
  81.3 56.4 %gather_grads.1 = (bf16[1,128,2048]{2,1,0:T(8,128)(2,1)}, bf16[1,128,2048]{2,1,0:T(8,128)(2,1)}, bf16[1,128,2048]{2,1,0:T(8,128)(2,1)}, f32[16]{0:T(128)}) custom-call(bf16[16,128,128]{2,1,0:T(8,128)(2,1)} %get-tuple-element.16.dq_in, f32[32,2,128,128]{3,2,1,0:T(8,128)} %get-tuple-element.17.own_in, bf16[32,2,128,128]{3,2,1,0:T(8,128)(2,1)} %get-tuple-element.18.oth_in, ...), custom_call_target="tpu_custom_call" | custom-call | tf_op jit(solution)/shard_map/gather_grads/pallas_call | solution.py:633
  137.7 2.2 %settle.1 = (bf16[1,128,2048]{2,1,0:T(8,128)(2,1)}, bf16[1,128,2048]{2,1,0:T(8,128)(2,1)}, bf16[1,128,2048]{2,1,0:T(8,128)(2,1)}, f32[16]{0:T(128)}) custom-call(bf16[1,128,2048]{2,1,0:T(8,128)(2,1)} %get-tuple-element.20.dq_in, bf16[1,128,2048]{2,1,0:T(8,128)(2,1)} %get-tuple-element.21.dk_in, bf16[1,128,2048]{2,1,0:T(8,128)(2,1)} %get-tuple-element.22.dv_in, ...), custom_call_target="tpu_custom_call" | custom-call | tf_op jit(solution)/shard_map/settle/pallas_call | solution.py:694

commit v4 on v3

--- a/solution.py
+++ b/solution.py
@@ -184,28 +184,39 @@
     return lax.dot_general(a, b, (((1,), (1,)), ((), ())), preferred_element_type=F32)
 
 
+def dot_tn(a, b):
+    return lax.dot_general(a, b, (((0,), (0,)), ((), ())), preferred_element_type=F32)
+
+
 def attend_kernel(
     ids_ref,
     soft_ref,
     span_ref,
+    qg_hbm,
+    kv_hbm,
+    dq_hbm,
+    own_hbm,
+    oth_hbm,
+    temper_ref,
     qg_ref,
-    kv_hbm,
     dq_ref,
-    own_ref,
     oth_ref,
-    temper_ref,
     k_sc,
     v_sc,
-    kt_sc,
     dk_acc,
     dv_acc,
     s_sc,
     d_sc,
-    p_sc,
+    w_sc,
+    u_sc,
     e_sc,
+    top_sc,
+    sum_sc,
     t_acc,
     slot_ref,
     count_ref,
+    order_ref,
+    place_ref,
     sems,
 ):
     _, _, col, core, inner, head, _, _ = place()
@@ -216,6 +227,9 @@
     scale = temper * inverse_root
     power = scale * log2e
 
+    take_qg = pltpu.make_async_copy(qg_hbm, qg_ref, sems.at[2])
+    take_qg.start()
+
     def clear(c):
         count_ref[c] = 0
 
@@ -232,18 +246,49 @@
         pltpu.make_async_copy(kv_hbm.at[b, 1], v_sc.at[rows], sems.at[1]).start()
 
     loop(BLOCKS, fetch)
+
+    def clear_rank(r):
+        place_ref[r] = 0
+
+    loop(MOST + 1, clear_rank)
+
+    def count_rank(i):
+        rank = slot_ref[member(i, inner, core)] % MOST
+        place_ref[rank + 1] = place_ref[rank + 1] + 1
+
+    loop(HEADS, count_rank)
+
+    def add_up(r):
+        place_ref[r + 1] = place_ref[r + 1] + place_ref[r]
+
+    loop(MOST, add_up)
+
+    def put_in_order(i):
+        rank = slot_ref[member(i, inner, core)] % MOST
+        at = place_ref[rank]
+        order_ref[at] = i
+        place_ref[rank] = at + 1
+
+    loop(HEADS, put_in_order)
     t_acc[...] = jnp.zeros_like(t_acc)
-
-    def zero(i):
-        rows = pl.ds(pl.multiple_of(i * BLK, BLK), BLK)
-        dk_acc[rows, :] = jnp.zeros((BLK, HD), F32)
-        dv_acc[rows, :] = jnp.zeros((BLK, HD), F32)
-
-    loop(NC * MOST, zero)
-    eye = (
-        lax.broadcasted_iota(jnp.int32, (HD, HD), 0)
-        == lax.broadcasted_iota(jnp.int32, (HD, HD), 1)
-    ).astype(BF16)
+    s_sc[...] = jnp.full_like(s_sc, OFF)
+    d_sc[...] = jnp.zeros_like(d_sc)
+    w_sc[...] = jnp.zeros_like(w_sc)
+    u_sc[...] = jnp.zeros_like(u_sc)
+    e_sc[...] = jnp.zeros_like(e_sc)
+    top_sc[...] = jnp.zeros_like(top_sc)
+    sum_sc[...] = jnp.zeros_like(sum_sc)
+
+    def rows_of(block):
+        return pl.ds(pl.multiple_of(slot_ref[block] * BLK, BLK), BLK)
+
+    def zero(group):
+        for j in range(4):
+            rows = rows_of(group * 4 + j)
+            dk_acc[rows, :] = jnp.zeros((BLK, HD), F32)
+            dv_acc[rows, :] = jnp.zeros((BLK, HD), F32)
+
+    loop(BLOCKS // 4, zero)
     gap = lax.broadcasted_iota(jnp.int32, (BLK, BLK), 0) - lax.broadcasted_iota(
         jnp.int32, (BLK, BLK), 1
     )
@@ -252,110 +297,160 @@
     pltpu.make_async_copy(v_sc.at[all_rows], v_sc.at[all_rows], sems.at[1]).wait()
 
     def blank(c):
-        @pl.when(count_ref[c] % 2 == 1)
-        def _():
-            rows = pl.ds(pl.multiple_of((c * MOST + count_ref[c]) * BLK, BLK), BLK)
+        def blank_slot(n):
+            rows = pl.ds(pl.multiple_of((c * MOST + count_ref[c] + n) * BLK, BLK), BLK)
             k_sc[rows, :] = jnp.zeros((BLK, HD), BF16)
             v_sc[rows, :] = jnp.zeros((BLK, HD), BF16)
-            kt_sc[:, rows] = jnp.zeros((HD, BLK), BF16)
+
+        loop(MOST - count_ref[c], blank_slot)
 
     loop(NC, blank)
 
-    def turn_keys(group):
-        for j in range(8):
-            start = pl.multiple_of(slot_ref[group * 8 + j] * BLK, BLK)
-            kt_sc[:, pl.ds(start, BLK)] = dot_nt(eye, k_sc[pl.ds(start, BLK), :]).astype(BF16)
-
-    loop(BLOCKS // 8, turn_keys)
-
-    def query_block(i, block, slot, cluster, rank, blocks):
-        rows = blocks * BLK
+    take_qg.wait()
+
+    tail = pl.ds(MOST * BLK, BLK)
+
+    def fold(x, how):
+        return how(x.reshape(x.shape[0] // 8, 8, BLK), axis=0)
+
+    def at_turn(n):
+        i = order_ref[jnp.clip(n, 0, HEADS - 1)]
+        block = member(i, inner, core)
+        slot = slot_ref[block]
+        before = jnp.maximum(block - 1, 0)
+        return i, block, slot, before
+
+    def spans(slot, before, blocks):
+        start = pl.multiple_of(slot // MOST * (MOST * BLK), BLK)
+        wstart = pl.multiple_of(slot_ref[before] * BLK, BLK)
+        return pl.ds(start, blocks * BLK), pl.ds(wstart, BLK)
+
+    def scores(n, blocks):
+        i, block, slot, before = at_turn(n)
+        span, wspan = spans(slot, before, blocks)
+        rank = slot % MOST
+        usable = (block >= 1) & (slot_ref[before] // MOST != slot // MOST)
+        edge = jnp.where(usable, BLK - width, 2 * BLK)
         q = qg_ref[i, 0]
         g = qg_ref[i, 1]
-        first = pl.multiple_of(cluster * (MOST * BLK), BLK)
-        span = pl.ds(first, rows)
-        before = jnp.maximum(block - 1, 0)
-        before_slot = slot_ref[before]
-        usable = (block >= 1) & (before_slot // MOST != cluster)
-        edge = jnp.where(usable, BLK - width, 2 * BLK)
-        wstart = pl.multiple_of(before_slot * BLK, BLK)
-        wspan = pl.ds(wstart, BLK)
+        raw = dot_nt(k_sc[span, :], q)
+        even = (blocks - 2) * BLK
         limit = (rank - blocks + 2) * BLK
-
-        s_sc[pl.ds(0, rows), :] = dot_nt(k_sc[span, :], q)
-        d_sc[pl.ds(0, rows), :] = dot_nt(v_sc[span, :], g)
-        s_win = jnp.where(gap > edge, dot_nt(k_sc[wspan, :], q), OFF)
-        s_sc[pl.ds(rows, BLK), :] = s_win
-        d_sc[pl.ds(rows, BLK), :] = dot_nt(v_sc[wspan, :], g)
-        for j in (blocks - 2, blocks - 1):
-            part = pl.ds(j * BLK, BLK)
-            shift = (j - blocks + 2) * BLK
-            s_sc[part, :] = jnp.where(gap <= limit - shift, s_sc[part, :], OFF)
-        top = jnp.full((8, BLK), OFF, F32)
-        for j in range(blocks + 1):
-            tile = s_sc[pl.ds(j * BLK, BLK), :]
-            top = jnp.maximum(top, jnp.max(tile.reshape(BLK // 8, 8, BLK), axis=0))
-        top = jnp.max(top, axis=0, keepdims=True)
-        total = jnp.zeros((8, BLK), F32)
-        mass = jnp.zeros((8, BLK), F32)
-        for j in range(blocks + 1):
-            part = pl.ds(j * BLK, BLK)
-            weight = jnp.exp2((s_sc[part, :] - top) * power)
-            p_sc[part, :] = weight
-            total = total + jnp.sum(weight.reshape(BLK // 8, 8, BLK), axis=0)
-            mass = mass + jnp.sum((weight * d_sc[part, :]).reshape(BLK // 8, 8, BLK), axis=0)
-        inverse = 1.0 / jnp.sum(total, axis=0, keepdims=True)
-        delta = jnp.sum(mass, axis=0, keepdims=True) * inverse
-        terms = jnp.zeros((8, BLK), F32)
-        for j in range(blocks + 1):
-            part = pl.ds(j * BLK, BLK)
-            prob = p_sc[part, :] * inverse
-            score = prob * (d_sc[part, :] - delta)
-            terms = terms + jnp.sum((score * s_sc[part, :]).reshape(BLK // 8, 8, BLK), axis=0)
-            e_sc[0, part, :] = prob.astype(BF16)
-            e_sc[1, part, :] = score.astype(BF16)
-        t_acc[...] += terms
-        body = pl.ds(0, rows)
-        tail = pl.ds(rows, BLK)
+        late = [jnp.where(gap <= limit - x * BLK, raw[even + x * BLK : even + (x + 1) * BLK], OFF) for x in (0, 1)]
+        near = jnp.where(gap > edge, dot_nt(k_sc[wspan, :], q), OFF)
+        top = fold(near, jnp.max)
+        for part in late:
+            top = jnp.maximum(top, fold(part, jnp.max))
+        if even:
+            s_sc[pl.ds(0, even), :] = raw[:even]
+            top = jnp.maximum(top, fold(raw[:even], jnp.max))
+        for x in (0, 1):
+            s_sc[pl.ds(even + x * BLK, BLK), :] = late[x]
+        s_sc[tail, :] = near
+        top_sc[...] = top
+        d_sc[pl.ds(0, blocks * BLK), :] = dot_nt(v_sc[span, :], g)
+        d_sc[tail, :] = dot_nt(v_sc[wspan, :], g)
+
+    def parts(blocks):
+        starts = [j * BLK + x for j in (*range(blocks), MOST) for x in range(0, BLK, 8)]
+        return [pl.ds(start, 8) for start in starts]
+
+    def weights(blocks):
+        top = jnp.max(top_sc[...], axis=0, keepdims=True)
+        sums = [jnp.zeros((8, BLK), F32) for _ in range(4)]
+        for part in parts(blocks):
+            raw = s_sc[part, :]
+            weight = jnp.exp2((raw - top) * power)
+            moment = weight * d_sc[part, :]
+            w_sc[part, :] = weight
+            u_sc[part, :] = moment
+            for x, term in enumerate((weight, moment, weight * raw, moment * raw)):
+                sums[x] = sums[x] + fold(term, jnp.sum)
+        for x in range(4):
+            sum_sc[x] = sums[x]
+
+    def shares(blocks):
+        total, mass, weight_raw, moment_raw = [jnp.sum(sum_sc[x], axis=0, keepdims=True) for x in range(4)]
+        inverse = jnp.where(total > 0.0, 1.0 / total, 0.0)
+        delta = mass * inverse
+        t_acc[...] += (moment_raw - delta * weight_raw) * inverse
+        for part in parts(blocks):
+            weight = w_sc[part, :]
+            e_sc[0, part, :] = (weight * inverse).astype(BF16)
+            e_sc[1, part, :] = ((u_sc[part, :] - weight * delta) * inverse).astype(BF16)
+
+    def products(n, blocks):
+        i, _, slot, before = at_turn(n)
+        span, wspan = spans(slot, before, blocks)
+        q = qg_ref[i, 0]
+        g = qg_ref[i, 1]
+        body = pl.ds(0, blocks * BLK)
+        grads = dot_tn(e_sc[1, body, :], k_sc[span, :])
+        grads += dot_tn(e_sc[1, tail, :], k_sc[wspan, :])
         dv_acc[span, :] += jnp.dot(e_sc[0, body, :], g, preferred_element_type=F32)
         dv_acc[wspan, :] += jnp.dot(e_sc[0, tail, :], g, preferred_element_type=F32)
         dk_acc[span, :] += jnp.dot(e_sc[1, body, :], q, preferred_element_type=F32)
         dk_acc[wspan, :] += jnp.dot(e_sc[1, tail, :], q, preferred_element_type=F32)
-        turned = jnp.dot(kt_sc[:, span], e_sc[1, body, :], preferred_element_type=F32)
-        turned += jnp.dot(kt_sc[:, wspan], e_sc[1, tail, :], preferred_element_type=F32)
-        dq_ref[i] = (turned * scale).T.astype(BF16)
-
-    def query_step(i):
-        block = member(i, inner, core)
-        slot = slot_ref[block]
-        cluster = slot // MOST
-        rank = slot % MOST
+        dq_ref[i] = (grads * scale).astype(BF16)
+
+    def by_size(n, work):
+        rank = at_turn(n)[2] % MOST
         for blocks in range(2, MOST + 1, 2):
 
             @pl.when(rank // 2 == blocks // 2 - 1)
             def _():
-                query_block(i, block, slot, cluster, rank, blocks)
-
-    loop(HEADS, query_step)
+                work(blocks)
+
+    def step(n):
+        def work(blocks):
+            products(n - 3, blocks)
+            shares(blocks)
+            weights(blocks)
+            scores(n, blocks)
+
+        by_size(n, work)
+
+    loop(HEADS, step)
+
+    def drain(blocks):
+        products(HEADS - 3, blocks)
+        shares(blocks)
+        weights(blocks)
+
+    by_size(HEADS - 1, drain)
+
+    def drain_more(blocks):
+        products(HEADS - 2, blocks)
+        shares(blocks)
+
+    by_size(HEADS - 1, drain_more)
+    by_size(HEADS - 1, lambda blocks: products(HEADS - 1, blocks))
+
+    pltpu.make_async_copy(dq_ref, dq_hbm, sems.at[2]).start()
 
     def give(i):
         at = out_turn(i % HEADS, col)
         owner = jnp.where(i < HEADS, 1 - inner, inner)
-        mine = pl.ds(pl.multiple_of(slot_ref[member(at, owner, core)] * BLK, BLK), BLK)
-        other = pl.ds(pl.multiple_of(slot_ref[member(at, owner, 1 - core)] * BLK, BLK), BLK)
-        own_ref[i, 0] = dk_acc[mine, :] * scale
-        own_ref[i, 1] = dv_acc[mine, :]
-        oth_ref[i, 0] = (dk_acc[other, :] * scale).astype(BF16)
+        mine = rows_of(member(at, owner, core))
+        other = rows_of(member(at, owner, 1 - core))
+        pltpu.make_async_copy(dk_acc.at[mine], own_hbm.at[i, 0], sems.at[0]).start()
+        pltpu.make_async_copy(dv_acc.at[mine], own_hbm.at[i, 1], sems.at[0]).start()
+        oth_ref[i, 0] = dk_acc[other, :].astype(BF16)
         oth_ref[i, 1] = dv_acc[other, :].astype(BF16)
+        pltpu.make_async_copy(oth_ref.at[i], oth_hbm.at[i], sems.at[1]).start()
 
     loop(CHIPS, give)
-    whole = jnp.sum(jnp.sum(t_acc[...], axis=0, keepdims=True), axis=1, keepdims=True)
+    whole = jnp.sum(t_acc[...], axis=1, keepdims=True)
     temper_ref[0] = jnp.broadcast_to(whole * inverse_root, (1, BLK))
+    pltpu.make_async_copy(dq_ref, dq_hbm, sems.at[2]).wait()
+    pltpu.make_async_copy(own_hbm, own_hbm, sems.at[0]).wait()
+    pltpu.make_async_copy(oth_ref, oth_hbm, sems.at[1]).wait()
 
 
 def attend(ids, soft, span, qg, kv):
     smem = pl.BlockSpec(memory_space=pltpu.SMEM)
     vmem = pl.BlockSpec(memory_space=pltpu.VMEM)
+    hbm = pl.BlockSpec(memory_space=pl.ANY)
     slots = NC * MOST * BLK
     return pl.pallas_call(
         attend_kernel,
@@ -365,34 +460,42 @@
             jax.ShapeDtypeStruct((CHIPS, 2, BLK, HD), BF16),
             jax.ShapeDtypeStruct((1, 1, BLK), F32),
         ),
-        in_specs=[smem, smem, smem, vmem, pl.BlockSpec(memory_space=pl.ANY)],
-        out_specs=(vmem, vmem, vmem, vmem),
+        in_specs=[smem, smem, smem, hbm, hbm],
+        out_specs=(hbm, hbm, hbm, vmem),
         scratch_shapes=[
+            pltpu.VMEM((HEADS, 2, BLK, HD), BF16),
+            pltpu.VMEM((HEADS, BLK, HD), BF16),
+            pltpu.VMEM((CHIPS, 2, BLK, HD), BF16),
             pltpu.VMEM((slots, HD), BF16),
             pltpu.VMEM((slots, HD), BF16),
-            pltpu.VMEM((HD, slots), BF16),
             pltpu.VMEM((slots, HD), F32),
             pltpu.VMEM((slots, HD), F32),
             pltpu.VMEM(((MOST + 1) * BLK, BLK), F32),
             pltpu.VMEM(((MOST + 1) * BLK, BLK), F32),
             pltpu.VMEM(((MOST + 1) * BLK, BLK), F32),
+            pltpu.VMEM(((MOST + 1) * BLK, BLK), F32),
             pltpu.VMEM((2, (MOST + 1) * BLK, BLK), BF16),
             pltpu.VMEM((8, BLK), F32),
+            pltpu.VMEM((4, 8, BLK), F32),
+            pltpu.VMEM((1, BLK), F32),
             pltpu.SMEM((BLOCKS,), jnp.int32),
             pltpu.SMEM((NC,), jnp.int32),
-            pltpu.SemaphoreType.DMA((2,)),
+            pltpu.SMEM((HEADS,), jnp.int32),
+            pltpu.SMEM((MOST + 1,), jnp.int32),
+            pltpu.SemaphoreType.DMA((3,)),
         ],
         name="attend",
     )(ids, soft, span, qg, kv)
 
 
-CHUNKS = 8
+CHUNKS = 16
 PER = CHIPS // CHUNKS
 HALF = CHUNKS // 2
 PEERS = DOCS * 4
 
 
 def gather_kernel(
+    soft_ref,
     dq_in,
     own_in,
     oth_in,
@@ -423,7 +526,14 @@
     me, row, col, core, inner, head, partner, neighbour = place()
     doc = lax.axis_index("dp")
     my_peer = doc * 4 + inner * 2 + core
+    scale = soft_ref[head] * (1.0 / math.sqrt(HD))
     barrier = pltpu.get_barrier_semaphore()
+
+    def mine(j):
+        part = pl.ds(j * PER, PER)
+        return pltpu.make_async_copy(own_in.at[part], own_v.at[part], own_sem.at[j])
+
+    loop(CHUNKS, lambda j: mine(j).start())
 
     def peer_id(j):
         half = row // 2
@@ -482,10 +592,6 @@
             device_id={"seq": partner},
         )
 
-    def mine(j):
-        part = pl.ds(j * PER, PER)
-        return pltpu.make_async_copy(own_in.at[part], own_v.at[part], own_sem.at[j])
-
     def near(u):
         part = pl.ds(u * PER, PER)
         return pltpu.make_async_remote_copy(
@@ -498,7 +604,6 @@
 
     def begin(j):
         theirs(j).start()
-        mine(j).start()
 
     loop(CHUNKS, begin)
     pltpu.make_async_copy(temper_in.at[0], t_heads.at[head], temper_recv.at[head]).start()
@@ -516,47 +621,18 @@
     loop(HEADS // 4, send_first)
 
     def give(u):
-        @pl.when(u < HALF)
-        def _():
-            mine(u).wait()
-            theirs(u).wait_recv()
-
-            def add_one(i):
-                for x in (0, 1):
-                    total = own_v[u * PER + i, x] + their_v[u * PER + i, x].astype(F32)
-                    give_v[u * PER + i, x] = total.astype(BF16)
-
-            loop(PER, add_one)
-
-        @pl.when(u > 0)
-        def _():
-            near(u - 1).start()
-
-    loop(HALF + 1, give)
-
-    def keep(u):
-        @pl.when(u < HALF)
-        def _():
-            mine(HALF + u).wait()
-            theirs(HALF + u).wait_recv()
-            near(u).wait_recv()
-
-            def add_one(i):
-                for x in (0, 1):
-                    at = (HALF + u) * PER + i
-                    total = own_v[at, x] + their_v[at, x].astype(F32)
-                    res_v[u * PER + i, x] = (total + near_v[u * PER + i, x].astype(F32)).astype(BF16)
-
-            loop(PER, add_one)
-
-        @pl.when(u > 0)
-        def _():
+        mine(u).wait()
+        theirs(u).wait_recv()
+
+        def add_one(i):
             for x in (0, 1):
-                for j in (0, 2, 1, 3):
-                    t = (u - 1) * PER + j
-                    go_home(out_turn(t, col), res_v.at[t, x], (dk_ref, dv_ref)[x], 1 + x)
-
-    loop(HALF + 1, keep)
+                total = own_v[u * PER + i, x] + their_v[u * PER + i, x].astype(F32)
+                give_v[u * PER + i, x] = total.astype(BF16)
+
+        loop(PER, add_one)
+        near(u).start()
+
+    loop(HALF, give)
 
     def heard(h):
         pltpu.make_async_copy(t_heads.at[h], t_heads.at[h], temper_recv.at[h]).wait()
@@ -581,6 +657,25 @@
 
     loop(PEERS, tell_peer)
 
+    def keep(u):
+        mine(HALF + u).wait()
+        theirs(HALF + u).wait_recv()
+        near(u).wait_recv()
+
+        def add_one(i):
+            for x in (0, 1):
+                at = (HALF + u) * PER + i
+                total = own_v[at, x] + their_v[at, x].astype(F32) + near_v[u * PER + i, x].astype(F32)
+                res_v[u * PER + i, x] = (total * scale if x == 0 else total).astype(BF16)
+
+        loop(PER, add_one)
+        for x in (0, 1):
+            for j in range(PER):
+                t = u * PER + j
+                go_home(out_turn(t, col), res_v.at[t, x], (dk_ref, dv_ref)[x], 1 + x)
+
+    loop(HALF, keep)
+
     def told(j):
         pltpu.make_async_copy(t_all.at[j], t_all.at[j], peer_recv.at[j]).wait()
 
@@ -625,7 +720,7 @@
     loop(HALF, close_near)
 
 
-def gather_grads(dq, own, oth, temper):
+def gather_grads(soft, dq, own, oth, temper):
     hbm = pl.BlockSpec(memory_space=pl.ANY)
     vmem = pl.BlockSpec(memory_space=pltpu.VMEM)
     whole = jax.ShapeDtypeStruct((1, BLK, HEADS * HD), BF16)
@@ -633,7 +728,7 @@
     return pl.pallas_call(
         gather_kernel,
         out_shape=(whole, whole, whole, jax.ShapeDtypeStruct((HEADS,), F32)),
-        in_specs=[hbm, hbm, hbm, vmem],
+        in_specs=[pl.BlockSpec(memory_space=pltpu.SMEM), hbm, hbm, hbm, vmem],
         out_specs=(hbm, hbm, hbm, pl.BlockSpec(memory_space=pltpu.SMEM)),
         scratch_shapes=[
             pltpu.VMEM((CHIPS, 2, BLK, HD), F32),
@@ -657,7 +752,7 @@
         ],
         compiler_params=pltpu.CompilerParams(collective_id=2, has_side_effects=True),
         name="gather_grads",
-    )(dq, own, oth, temper)
+    )(soft, dq, own, oth, temper)
 
 
 PARTS = 2
@@ -708,7 +803,7 @@
 def shards(q, k, v, g, softness, grouping, span):
     qg, kv = scatter_blocks(q, k, v, g)
     dq, own, oth, temper = attend(grouping.reshape(HEADS, BLOCKS), softness, span, qg, kv)
-    return settle(*gather_grads(dq, own, oth, temper))
+    return settle(*gather_grads(softness, dq, own, oth, temper))
 
 
 def solution(mesh):

time: 140 us -> 131 us (0.936)
  Pallas kernels: 139 us -> 130 us
    pallas_call x1, Pallas kernels: 26.5 us -> 19.5 us  [attend(): pl.pallas_call(attend_kernel, out_shape=(jax.ShapeDtypeStruct((HEADS, BLK...]
    pallas_call x1, Pallas kernels: 56.4 us -> 54.5 us  [gather_grads(): pl.pallas_call(gather_kernel, out_shape=(whole, whole, whole, jax.ShapeDt...]
where the time goes in v4:
time: 131 us
  Pallas kernels  130 us (99%)
    pallas_call x1, Pallas kernels, gather_grads(): pl.pallas_call(gather_kernel, out_shape=(whole, whole, whole, jax.ShapeDt...  54.5 us
    pallas_call x1, Pallas kernels, scatter_blocks(): pl.pallas_call(scatter_kernel, out_shape=(jax.ShapeDtypeStruct((HEADS, 2,...  54.1 us
    pallas_call x1, Pallas kernels, attend(): pl.pallas_call(attend_kernel, out_shape=(jax.ShapeDtypeStruct((HEADS, BLK...  19.5 us

profile of v4, /device:TPU:1, one launch (start us, length us, event | category | flops | bytes accessed | tf_op | source)
XLA Modules:
  0.0 131.2 jit_solution(8971945572009832154)
XLA Ops:
  0.6 54.1 %scatter_blocks.1 = (bf16[16,2,128,128]{3,2,1,0:T(8,128)(2,1)}, bf16[64,2,128,128]{3,2,1,0:T(8,128)(2,1)}) custom-call(bf16[1,128,2048]{2,1,0:T(8,128)(2,1)} %q_ref.1, bf16[1,128,2048]{2,1,0:T(8,128)(2,1)} %k_ref.1, bf16[1,128,2048]{2,1,0:T(8,128)(2,1)} %v_ref.1, bf16[1,128,2048]{2,1,0:T(8,128)(2,1)} %g_ref.1), custom_call_target="tpu_custom_call" | custom-call | tf_op jit(solution)/shard_map/scatter_blocks/pallas_call | solution.py:168
  54.8 19.5 %attend.1 = (bf16[16,128,128]{2,1,0:T(8,128)(2,1)}, f32[32,2,128,128]{3,2,1,0:T(8,128)}, bf16[32,2,128,128]{3,2,1,0:T(8,128)(2,1)}, f32[1,1,128]{2,1,0:T(1,128)}) custom-call(s32[16,64]{1,0:T(8,128)} %bitcast.1, f32[16]{0:T(128)} %soft_ref.3, s32[16]{0:T(128)} %span_ref.1, bf16[16,2,128,128]{3,2,1,0:T(8,128)(2,1)} %get-tuple-element.14.qg_hbm, ...), custom_call_target="tpu_custom_call" | custom-call | tf_op jit(solution)/shard_map/attend/pallas_call | solution.py:455
  74.3 54.5 %gather_grads.1 = (bf16[1,128,2048]{2,1,0:T(8,128)(2,1)}, bf16[1,128,2048]{2,1,0:T(8,128)(2,1)}, bf16[1,128,2048]{2,1,0:T(8,128)(2,1)}, f32[16]{0:T(128)}) custom-call(f32[16]{0:T(128)} %soft_ref.3, bf16[16,128,128]{2,1,0:T(8,128)(2,1)} %get-tuple-element.16.dq_in, f32[32,2,128,128]{3,2,1,0:T(8,128)} %get-tuple-element.17.own_in, ...), custom_call_target="tpu_custom_call" | custom-call | tf_op jit(solution)/shard_map/gather_grads/pallas_call | solution.py:728
  128.9 2.2 %settle.1 = (bf16[1,128,2048]{2,1,0:T(8,128)(2,1)}, bf16[1,128,2048]{2,1,0:T(8,128)(2,1)}, bf16[1,128,2048]{2,1,0:T(8,128)(2,1)}, f32[16]{0:T(128)}) custom-call(bf16[1,128,2048]{2,1,0:T(8,128)(2,1)} %get-tuple-element.20.dq_in, bf16[1,128,2048]{2,1,0:T(8,128)(2,1)} %get-tuple-element.21.dk_in, bf16[1,128,2048]{2,1,0:T(8,128)(2,1)} %get-tuple-element.22.dv_in, ...), custom_call_target="tpu_custom_call" | custom-call | tf_op jit(solution)/shard_map/settle/pallas_call | solution.py:789

commit v5 on v4

--- a/solution.py
+++ b/solution.py
@@ -244,6 +244,14 @@
         rows = pl.ds(pl.multiple_of(slot * BLK, BLK), BLK)
         pltpu.make_async_copy(kv_hbm.at[b, 0], k_sc.at[rows], sems.at[0]).start()
         pltpu.make_async_copy(kv_hbm.at[b, 1], v_sc.at[rows], sems.at[1]).start()
+        dk_acc[rows, :] = jnp.zeros((BLK, HD), F32)
+        dv_acc[rows, :] = jnp.zeros((BLK, HD), F32)
+        part = pl.ds(pl.multiple_of(jnp.minimum(b, (MOST + 1) * BLK // 32 - 1) * 32, 32), 32)
+        s_sc[part, :] = jnp.full((32, BLK), OFF, F32)
+        for ref in (d_sc, w_sc, u_sc):
+            ref[part, :] = jnp.zeros((32, BLK), F32)
+        for x in (0, 1):
+            e_sc[x, part, :] = jnp.zeros((32, BLK), BF16)
 
     loop(BLOCKS, fetch)
 
@@ -271,24 +279,12 @@
 
     loop(HEADS, put_in_order)
     t_acc[...] = jnp.zeros_like(t_acc)
-    s_sc[...] = jnp.full_like(s_sc, OFF)
-    d_sc[...] = jnp.zeros_like(d_sc)
-    w_sc[...] = jnp.zeros_like(w_sc)
-    u_sc[...] = jnp.zeros_like(u_sc)
-    e_sc[...] = jnp.zeros_like(e_sc)
     top_sc[...] = jnp.zeros_like(top_sc)
     sum_sc[...] = jnp.zeros_like(sum_sc)
 
     def rows_of(block):
         return pl.ds(pl.multiple_of(slot_ref[block] * BLK, BLK), BLK)
 
-    def zero(group):
-        for j in range(4):
-            rows = rows_of(group * 4 + j)
-            dk_acc[rows, :] = jnp.zeros((BLK, HD), F32)
-            dv_acc[rows, :] = jnp.zeros((BLK, HD), F32)
-
-    loop(BLOCKS // 4, zero)
     gap = lax.broadcasted_iota(jnp.int32, (BLK, BLK), 0) - lax.broadcasted_iota(
         jnp.int32, (BLK, BLK), 1
     )

time: 131 us -> 131 us (level)
  no operation moved by 1% of the time
where the time goes in v5:
time: 131 us
  Pallas kernels  130 us (99%)
    pallas_call x1, Pallas kernels, scatter_blocks(): pl.pallas_call(scatter_kernel, out_shape=(jax.ShapeDtypeStruct((HEADS, 2,...  54.1 us
    pallas_call x1, Pallas kernels, gather_grads(): pl.pallas_call(gather_kernel, out_shape=(whole, whole, whole, jax.ShapeDt...  53.4 us
    pallas_call x1, Pallas kernels, attend(): pl.pallas_call(attend_kernel, out_shape=(jax.ShapeDtypeStruct((HEADS, BLK...  20.5 us

profile of v5, /device:TPU:1, one launch (start us, length us, event | category | flops | bytes accessed | tf_op | source)
XLA Modules:
  0.0 131.0 jit_solution(6721962309318979189)
XLA Ops:
  0.6 54.1 %scatter_blocks.1 = (bf16[16,2,128,128]{3,2,1,0:T(8,128)(2,1)}, bf16[64,2,128,128]{3,2,1,0:T(8,128)(2,1)}) custom-call(bf16[1,128,2048]{2,1,0:T(8,128)(2,1)} %q_ref.1, bf16[1,128,2048]{2,1,0:T(8,128)(2,1)} %k_ref.1, bf16[1,128,2048]{2,1,0:T(8,128)(2,1)} %v_ref.1, bf16[1,128,2048]{2,1,0:T(8,128)(2,1)} %g_ref.1), custom_call_target="tpu_custom_call" | custom-call | tf_op jit(solution)/shard_map/scatter_blocks/pallas_call | solution.py:168
  54.8 20.5 %attend.1 = (bf16[16,128,128]{2,1,0:T(8,128)(2,1)}, f32[32,2,128,128]{3,2,1,0:T(8,128)}, bf16[32,2,128,128]{3,2,1,0:T(8,128)(2,1)}, f32[1,1,128]{2,1,0:T(1,128)}) custom-call(s32[16,64]{1,0:T(8,128)} %bitcast.1, f32[16]{0:T(128)} %soft_ref.3, s32[16]{0:T(128)} %span_ref.1, bf16[16,2,128,128]{3,2,1,0:T(8,128)(2,1)} %get-tuple-element.14.qg_hbm, ...), custom_call_target="tpu_custom_call" | custom-call | tf_op jit(solution)/shard_map/attend/pallas_call | solution.py:451
  75.2 53.4 %gather_grads.1 = (bf16[1,128,2048]{2,1,0:T(8,128)(2,1)}, bf16[1,128,2048]{2,1,0:T(8,128)(2,1)}, bf16[1,128,2048]{2,1,0:T(8,128)(2,1)}, f32[16]{0:T(128)}) custom-call(f32[16]{0:T(128)} %soft_ref.3, bf16[16,128,128]{2,1,0:T(8,128)(2,1)} %get-tuple-element.16.dq_in, f32[32,2,128,128]{3,2,1,0:T(8,128)} %get-tuple-element.17.own_in, ...), custom_call_target="tpu_custom_call" | custom-call | tf_op jit(solution)/shard_map/gather_grads/pallas_call | solution.py:724
  128.6 2.2 %settle.1 = (bf16[1,128,2048]{2,1,0:T(8,128)(2,1)}, bf16[1,128,2048]{2,1,0:T(8,128)(2,1)}, bf16[1,128,2048]{2,1,0:T(8,128)(2,1)}, f32[16]{0:T(128)}) custom-call(bf16[1,128,2048]{2,1,0:T(8,128)(2,1)} %get-tuple-element.20.dq_in, bf16[1,128,2048]{2,1,0:T(8,128)(2,1)} %get-tuple-element.21.dk_in, bf16[1,128,2048]{2,1,0:T(8,128)(2,1)} %get-tuple-element.22.dv_in, ...), custom_call_target="tpu_custom_call" | custom-call | tf_op jit(solution)/shard_map/settle/pallas_call | solution.py:785
